TPU v7x, 512 devices: a whole 4x4x16 slice. The times are simulated.
512 devices in a mesh: dp: 2 (over core), row: 16 (over y, z_lo), col: 16 (over z_hi, x).
Axes of the slice: x: 4, y: 4, z: 16 (z_hi: 4, z_lo: 4; z = z_hi * 4 + z_lo), core: 2. Of those that a mesh axis runs over, the one named last changes fastest.
Arguments:
- queries: bfloat16 [2, 2048, 4096], P('dp', 'row', 'col'), may hold values from -6 to 6
- key_vectors: bfloat16 [2, 2048, 4096], P('dp', 'row', 'col'), may hold values from -6 to 6
- value_vectors: bfloat16 [2, 2048, 4096], P('dp', 'row', 'col'), may hold values from -6 to 6
- out_weight: bfloat16 [4096, 3072], P('row', 'col'), may hold values from -0.09375 to 0.09375
- out_grad: bfloat16 [2, 2048, 3072], P('dp', 'row', 'col'), may hold values from -6 to 6
Outputs:
- output: bfloat16 [2, 2048, 3072], P('dp', 'row', 'col')
- grad_queries: bfloat16 [2, 2048, 4096], P('dp', 'row', 'col')
- grad_keys: bfloat16 [2, 2048, 4096], P('dp', 'row', 'col')
- grad_values: bfloat16 [2, 2048, 4096], P('dp', 'row', 'col')
- grad_weight: float32 [4096, 3072], P(('dp', 'row'), 'col')
All inputs are finite; a program needn't handle non-finite values.
Results may differ from a plain program's by a relative error of at most 0.038.
Values may be sent and summed in bfloat16 or wider, within the bound.
A program may use at most 64 MiB of HBM per device.

v0:
```python
import math

import jax
import jax.numpy as jnp
from jax import lax
from jax.sharding import PartitionSpec as P

HEAD = 128


NEG = -1e30


def split_heads(array_in):
    return array_in.reshape(array_in.shape[0], array_in.shape[1] // HEAD, HEAD)


def merge_heads(array_in):
    return array_in.reshape(array_in.shape[0], array_in.shape[1] * array_in.shape[2])


def causal_scores(query_part, key_part, query_first, key_first):
    scores = jnp.einsum(
        "qhe,khe->qhk", query_part, key_part, preferred_element_type=jnp.float32
    ) * (1.0 / math.sqrt(HEAD))
    query_pos = query_first + lax.broadcasted_iota(jnp.int32, (query_part.shape[0], 1, 1), 0)
    key_pos = key_first + lax.broadcasted_iota(jnp.int32, (1, 1, key_part.shape[0]), 2)
    visible = key_pos <= query_pos
    return (jnp.where(visible, scores, NEG), visible)


def shards(queries, key_vectors, value_vectors, out_weight, out_grad):
    own_rows = queries.shape[1]
    heads_local = queries.shape[2] // HEAD
    own_first = lax.axis_index("row") * own_rows
    own_queries = split_heads(queries[0])
    own_keys = split_heads(key_vectors[0])
    own_values = split_heads(value_vectors[0])
    grad_local = out_grad[0]
    portion = (
        lax.all_gather(key_vectors[0], "row", axis=0, tiled=True),
        lax.all_gather(value_vectors[0], "row", axis=0, tiled=True),
    )
    running_max = jnp.full((own_rows, heads_local), NEG, jnp.float32)
    key_part = split_heads(portion[0])
    value_part = split_heads(portion[1]).astype(jnp.float32)
    scores, visible = causal_scores(own_queries, key_part, own_first, jnp.int32(0))
    new_max = jnp.maximum(running_max, jnp.max(scores, axis=2))
    weights = jnp.where(visible, jnp.exp(scores - new_max[:, :, None]), 0.0)
    running_sum = jnp.sum(weights, axis=2)
    accumulated = jnp.einsum(
        "qhk,khe->qhe",
        weights,
        value_part,
        precision=lax.Precision.HIGHEST,
        preferred_element_type=jnp.float32,
    )
    running_max, running_sum, accumulated = (new_max, running_sum, accumulated)
    attended = merge_heads(accumulated / running_sum[:, :, None]).astype(jnp.bfloat16)
    log_norm = running_max + jnp.log(running_sum)
    attn_full = lax.all_gather(attended, "col", axis=1, tiled=True)
    columns = attn_full
    output_rows = jnp.dot(
        columns,
        lax.all_gather(out_weight, "row", axis=0, tiled=True),
        preferred_element_type=jnp.float32,
    )
    head_terms = lax.dot_general(
        grad_local,
        lax.all_gather(out_weight, "row", axis=0, tiled=True),
        (((1,), (1,)), ((), ())),
        preferred_element_type=jnp.float32,
    )
    grad_attended = lax.psum_scatter(
        head_terms.astype(jnp.bfloat16), "col", scatter_dimension=1, tiled=True
    )
    upstream_own = split_heads(grad_attended)
    row_dot = jnp.sum(
        upstream_own.astype(jnp.float32) * split_heads(attended).astype(jnp.float32), axis=2
    )
    portion = (
        lax.all_gather(key_vectors[0], "row", axis=0, tiled=True),
        lax.all_gather(value_vectors[0], "row", axis=0, tiled=True),
    )
    key_part = split_heads(portion[0])
    value_part = split_heads(portion[1])
    scores, visible = causal_scores(own_queries, key_part, own_first, jnp.int32(0))
    attention = jnp.where(visible, jnp.exp(scores - log_norm[:, :, None]), 0.0)
    grad_probs = jnp.einsum(
        "qhe,khe->qhk", upstream_own, value_part, preferred_element_type=jnp.float32
    )
    grad_scores = (attention * (grad_probs - row_dot[:, :, None])).astype(jnp.bfloat16)
    grad_query_sum = jnp.einsum(
        "qhk,khe->qhe", grad_scores, key_part, preferred_element_type=jnp.float32
    )
    grad_queries = merge_heads(grad_query_sum * (1.0 / math.sqrt(HEAD))).astype(jnp.bfloat16)
    sent = (queries[0].astype(jnp.float32), grad_attended.astype(jnp.float32), log_norm, row_dot)
    portion = (
        lax.all_gather(sent[0], "row", axis=0, tiled=True),
        lax.all_gather(sent[1], "row", axis=0, tiled=True),
        lax.all_gather(sent[2], "row", axis=0, tiled=True),
        lax.all_gather(sent[3], "row", axis=0, tiled=True),
    )
    query_part = split_heads(portion[0].astype(jnp.bfloat16))
    upstream = split_heads(portion[1].astype(jnp.bfloat16))
    norm_part = portion[2]
    dot_part = portion[3]
    scores, visible = causal_scores(query_part, own_keys, jnp.int32(0), own_first)
    attention = jnp.where(visible, jnp.exp(scores - norm_part[:, :, None]), 0.0)
    grad_value_sum = jnp.einsum(
        "qhk,qhe->khe", attention.astype(jnp.bfloat16), upstream, preferred_element_type=jnp.float32
    )
    grad_probs = jnp.einsum(
        "qhe,khe->qhk", upstream, own_values, preferred_element_type=jnp.float32
    )
    grad_scores = (attention * (grad_probs - dot_part[:, :, None])).astype(jnp.bfloat16)
    grad_key_sum = jnp.einsum(
        "qhk,qhe->khe", grad_scores, query_part, preferred_element_type=jnp.float32
    )
    grad_key_sum, grad_value_sum = (grad_key_sum, grad_value_sum)
    grad_keys = merge_heads(grad_key_sum * (1.0 / math.sqrt(HEAD))).astype(jnp.bfloat16)
    grad_values = merge_heads(grad_value_sum).astype(jnp.bfloat16)
    columns = attn_full
    grad_weight = lax.psum_scatter(
        lax.dot_general(
            columns, grad_local, (((0,), (0,)), ((), ())), preferred_element_type=jnp.float32
        ),
        ("dp", "row"),
        scatter_dimension=0,
        tiled=True,
    )
    return (
        output_rows.astype(jnp.bfloat16)[None],
        grad_queries[None],
        grad_keys[None],
        grad_values[None],
        grad_weight,
    )


def solution(mesh):
    return jax.shard_map(
        shards,
        mesh=mesh,
        in_specs=(
            P("dp", "row", "col"),
            P("dp", "row", "col"),
            P("dp", "row", "col"),
            P("row", "col"),
            P("dp", "row", "col"),
        ),
        out_specs=(
            P("dp", "row", "col"),
            P("dp", "row", "col"),
            P("dp", "row", "col"),
            P("dp", "row", "col"),
            P(("dp", "row"), "col"),
        ),
        check_vma=False,
    )
```

profile of v0, /device:TPU:1, one launch (start us, length us, event | category | flops | bytes accessed | tf_op | source)
XLA Modules:
  0.0 794.0 jit_solution(7137687552195433287)
XLA Ops:
  7.2 0.0 all-gather.12.cloned.1.call-start
  7.2 0.7 all-gather.12.cloned.1.call-update
  7.9 0.0 all-gather.18.cloned.1.call-start
  8.0 0.7 all-gather.18.cloned.1.call-update
  8.7 0.0 all-gather.16.cloned.1.call-start
  8.7 1.6 copy.24
  10.3 0.0 all-gather.16.cloned.1.call-update
  10.3 0.0 reduce-scatter.3.cloned.1.call-start
  10.4 78.9 %all-gather.12.cloned.1.call-done = bf16[4096,192]{0,1:T(8,128)(2,1)} async-done(((bf16[256,192]{0,1:T(8,128)(2,1)}), bf16[4096,192]{0,1:T(8,128)(2,1)}) %all-gather.12.cloned.1.call-update) | async-done | bytes 1572880 | tf_op jit(solution)/shard_map/all_gather | solution.py:65
  89.2 2.8 convolution_convert_fusion
  92.1 0.0 reduce-scatter.3.cloned.1.call-update
  92.1 0.0 all-gather.10.cloned.1.call-start
  92.2 0.2 iota_compare_fusion.1
  92.4 85.0 %all-gather.18.cloned.1.call-done = bf16[1,2048,256]{2,1,0:T(8,128)(2,1)} async-done(((bf16[1,128,256]{2,1,0:T(8,128)(2,1)}), bf16[1,2048,256]{2,1,0:T(8,128)(2,1)}) %all-gather.18.cloned.1.call-update) | async-done | bytes 1048592 | tf_op jit(solution)/shard_map/all_gather | solution.py:42
  177.4 1.5 copy.27
  178.9 76.4 %all-gather.16.cloned.1.call-done = bf16[1,2048,256]{1,2,0:T(8,128)(2,1)} async-done(((bf16[1,128,256]{1,2,0:T(8,128)(2,1)}), bf16[1,2048,256]{1,2,0:T(8,128)(2,1)}) %all-gather.16.cloned.1.call-update) | async-done | bytes 1048592 | tf_op jit(solution)/shard_map/all_gather | solution.py:41
  255.2 1.9 fusion.41
  257.1 0.4 fusion.13
  257.6 122.3 %reduce-scatter.3.cloned.1.call-done = bf16[128,256]{1,0:T(8,128)(2,1)} async-done(((bf16[128,4096]{1,0:T(8,128)(2,1)}), bf16[128,256]{1,0:T(8,128)(2,1)}) %reduce-scatter.3.cloned.1.call-update) | async-done | bytes 65552 | tf_op jit(solution)/shard_map/reduce_scatter | solution.py:74
  379.9 1.6 copy.29
  381.4 3.1 multiply_reduce_fusion
  384.6 0.0 all-gather.10.cloned.1.call-update
  384.6 0.0 all-gather.20.cloned.1.call-start
  384.6 0.7 copy.31
  385.4 0.0 all-gather.20.cloned.1.call-update
  385.4 0.0 all-gather.14.cloned.1.call-start
  385.5 0.7 all-gather.14.cloned.1.call-update
  386.2 0.0 reduce-scatter.5.cloned.1.call-start
  386.2 71.2 %all-gather.10.cloned.1.call-done = bf16[128,4096]{0,1:T(8,128)(2,1)} async-done(((bf16[128,256]{0,1:T(8,128)(2,1)}), bf16[128,4096]{0,1:T(8,128)(2,1)}) %all-gather.10.cloned.1.call-update) | async-done | bytes 1048592 | tf_op jit(solution)/shard_map/all_gather | solution.py:61
  457.4 3.4 fusion.36
  460.9 0.8 copy-done.6
  461.7 0.6 reshape_squeeze.10
  462.3 0.1 copy.48
  462.4 0.9 iota_compare_fusion
  463.4 33.1 %all_gather.32 = f32[2048,2]{0,1:T(2,128)S(1)} all-gather(f32[128,2]{0,1:T(2,128)S(1)} %log_add_fusion), channel_id=1, replica_groups=mesh['dp'=2,'row'=16,'col'=16] {'row'}, dimensions={0}, use_global_device_ids=true | all-gather | bytes 17408 | tf_op jit(solution)/shard_map/all_gather | solution.py:101
  496.4 25.6 %all-gather.20.cloned.1.call-done = bf16[1,2048,256]{1,2,0:T(8,128)(2,1)} async-done(((bf16[1,128,256]{1,2,0:T(8,128)(2,1)}), bf16[1,2048,256]{1,2,0:T(8,128)(2,1)}) %all-gather.20.cloned.1.call-update) | async-done | bytes 1048592 | tf_op jit(solution)/shard_map/all_gather | solution.py:99
  522.1 3.6 fusion.8
  525.6 3.0 fusion.21
  528.7 1.7 copy.37
  530.4 35.5 %all_gather.34 = f32[2048,2]{0,1:T(2,128)S(1)} all-gather(f32[128,2]{0,1:T(2,128)S(1)} %get-tuple-element.17), channel_id=1, replica_groups=mesh['dp'=2,'row'=16,'col'=16] {'row'}, dimensions={0}, use_global_device_ids=true | all-gather | bytes 17408 | tf_op jit(solution)/shard_map/all_gather | solution.py:102
  565.9 44.3 %all-gather.14.cloned.1.call-done = bf16[2048,256]{1,0:T(8,128)(2,1)} async-done(((bf16[128,256]{1,0:T(8,128)(2,1)}), bf16[2048,256]{1,0:T(8,128)(2,1)}) %all-gather.14.cloned.1.call-update) | async-done | bytes 1048592 | tf_op jit(solution)/shard_map/all_gather | solution.py:100
  610.2 1.5 copy.49
  611.7 2.0 fusion.23
  613.7 0.7 copy.38
  614.4 0.4 convolution_convert_fusion.1
  614.9 0.7 copy.39
  615.6 2.9 fusion.24
  618.5 168.6 %reduce-scatter.5.cloned.1.call-done = f32[128,192]{0,1:T(8,128)} async-done(((f32[4096,192]{0,1:T(8,128)}), f32[128,192]{0,1:T(8,128)}) %reduce-scatter.5.cloned.1.call-update) | async-done | bytes 98320 | tf_op jit(solution)/shard_map/reduce_scatter | solution.py:124
  (20 shorter events, 0.1 us)
Async XLA Ops:
  7.2 82.1 %copy-start = (bf16[1,128,192]{1,2,0:T(8,128)(2,1)S(1)}, bf16[1,128,192]{1,2,0:T(8,128)(2,1)}, u32[]{:S(2)}) copy-start(bf16[1,128,192]{1,2,0:T(8,128)(2,1)} %param.9) | copy-start | bytes 147460
  7.2 85.0 %copy-start.4 = (bf16[1,128,256]{2,1,0:T(8,128)(2,1)S(1)}, bf16[1,128,256]{2,1,0:T(8,128)(2,1)}, u32[]{:S(2)}) copy-start(bf16[1,128,256]{2,1,0:T(8,128)(2,1)} %param.5) | copy-start | bytes 196612
  7.2 82.0 %all-gather.12.cloned.1.call-start = ((), (), s32[]{:S(2)}) async-start(), calls=%async_computation.3 | async-start | bytes 1671168 | tf_op jit(solution)/shard_map/all_gather | solution.py:65
  7.9 169.4 %all-gather.18.cloned.1.call-start = ((), (), s32[]{:S(2)}) async-start(), calls=%async_computation.8 | async-start | bytes 1114112 | tf_op jit(solution)/shard_map/all_gather | solution.py:42
  8.7 246.6 %all-gather.16.cloned.1.call-start = ((), (), s32[]{:S(2)}) async-start(), calls=%async_computation.7 | async-start | bytes 1114112 | tf_op jit(solution)/shard_map/all_gather | solution.py:41
  10.3 369.5 %reduce-scatter.3.cloned.1.call-start = ((), (), s32[]{:S(2)}) async-start(), calls=%async_computation.4 | async-start | bytes 1114112 | tf_op jit(solution)/shard_map/reduce_scatter | solution.py:74
  92.1 365.3 %all-gather.10.cloned.1.call-start = ((), (), s32[]{:S(2)}) async-start(), calls=%async_computation.2 | async-start | bytes 1114112 | tf_op jit(solution)/shard_map/all_gather | solution.py:61
  178.9 202.6 %copy-start.3 = (bf16[1,2048,256]{1,2,0:T(8,128)(2,1)}, bf16[1,2048,256]{1,2,0:T(8,128)(2,1)S(1)}, u32[]{:S(2)}) copy-start(bf16[1,2048,256]{1,2,0:T(8,128)(2,1)S(1)} %copy.27) | copy-start | bytes 3145732
  381.4 3.2 copy-start.5
  384.6 137.5 %all-gather.20.cloned.1.call-start = ((), (), s32[]{:S(2)}) async-start(), calls=%async_computation.9 | async-start | bytes 1114112 | tf_op jit(solution)/shard_map/all_gather | solution.py:99
  385.4 224.8 %all-gather.14.cloned.1.call-start = ((), (), s32[]{:S(2)}) async-start(), calls=%async_computation.5 | async-start | bytes 1114112 | tf_op jit(solution)/shard_map/all_gather | solution.py:100
  386.2 401.0 %reduce-scatter.5.cloned.1.call-start = ((), (), s32[]{:S(2)}) async-start(), calls=%async_computation.6 | async-start | bytes 3244032 | tf_op jit(solution)/shard_map/reduce_scatter | solution.py:124
  460.8 0.8 copy-start.6
  460.8 1.5 copy-start.7
  522.1 3.6 copy-start.2
  528.7 83.0 %copy-start.1 = (f32[2048,2,128]{0,2,1:T(8,128)S(1)}, f32[2048,2,128]{0,2,1:T(8,128)}, u32[]{:S(2)}) copy-start(f32[2048,2,128]{0,2,1:T(8,128)} %fusion.8) | copy-start | bytes 6291460
Sparse Core Ops, SparseCore 0:
  10.0 79.1 all-gather.11
  91.3 86.0 all-gather.17
  179.9 75.2 all-gather.15
  259.2 120.6 reduce-scatter.2
  384.7 72.6 all-gather.9
  460.0 61.9 all-gather.19
  524.4 85.7 all-gather.13
  613.8 173.2 reduce-scatter.4
where the time goes:
time: 795 us; the launch traced here: 794 us
  waiting for transfers between devices  674 us (85%)
  blocking collectives  68.5 us (9%)
  matrix products  23.2 us (3%)
  between operations  14.3 us (2%)
  local copies, waits for them, and re-layouts  11.7 us (1%)
    reduce_scatter x1, waiting for transfers between devices, shards(): lax.psum_scatter(lax.dot_general(columns, grad_local, (((0,), (0,)), ((),...  169 us
    reduce_scatter x1, waiting for transfers between devices, shards(): lax.psum_scatter(head_terms.astype(jnp.bfloat16), 'col', scatter_dimensio...  122 us
    all_gather x1, waiting for transfers between devices, shards(): lax.all_gather(value_vectors[0], 'row', axis=0, tiled=True)  85 us
    all_gather x1, waiting for transfers between devices, shards(): lax.all_gather(out_weight, 'row', axis=0, tiled=True)  78.9 us
    all_gather x1, waiting for transfers between devices, shards(): lax.all_gather(key_vectors[0], 'row', axis=0, tiled=True)  76.4 us
    all_gather x1, waiting for transfers between devices, shards(): attn_full = lax.all_gather(attended, 'col', axis=1, tiled=True)  71.2 us
    all_gather x1, waiting for transfers between devices, shards(): lax.all_gather(sent[1], 'row', axis=0, tiled=True)  44.3 us
    all_gather x1, blocking collectives, shards(): lax.all_gather(sent[3], 'row', axis=0, tiled=True)  35.5 us
  transfers between devices with their start and end apart: 8, of which 8 were waited for; matrix products, arithmetic and copies ran while one was open for 4% of the time, Pallas kernels for 0%

commit v1 on v0

v1 whole, which is shorter than its diff:
```python
import functools
import math

import jax
import jax.numpy as jnp
from jax import lax
from jax.experimental import pallas as pl
from jax.experimental.pallas import tpu as pltpu
from jax.sharding import PartitionSpec as P

HEAD = 128
NEG = -1e30
SCALE = 1.0 / math.sqrt(HEAD)
F32 = jnp.float32
BF16 = jnp.bfloat16
NT = (((1,), (1,)), ((), ()))


def dot(a, b):
    return jnp.dot(a, b, preferred_element_type=F32)


def dot_nt(a, b):
    return lax.dot_general(a, b, NT, preferred_element_type=F32)


def kernel(
    n,
    rows,
    cols,
    q_ref,
    k_ref,
    v_ref,
    wt_ref,
    g_ref,
    gt_ref,
    out_ref,
    dq_ref,
    dk_ref,
    dv_ref,
    gw_ref,
    kf,
    vf,
    qf,
    df,
    st,
    wf,
    hs,
    hx,
    hz,
    hr,
    of,
    gp,
    gd,
    gy,
    gyr,
    gz,
    gzr,
    send_sems,
    recv_sems,
):
    dp, row, col = lax.axis_index("dp"), lax.axis_index("row"), lax.axis_index("col")
    y, z = row // n, lax.rem(row, n)
    u, x = col // n, lax.rem(col, n)
    chunk = n * rows
    others = list(range(1, n))
    far = sorted(others, key=lambda d: -min(d, n - d))

    def at(base, d):
        return lax.rem(base + d + n, n)

    dp_peer = {"dp": 1 - dp}

    def z_peer(d):
        return {"row": y * n + at(z, d)}

    def y_peer(d):
        return {"row": at(y, d) * n + z}

    def u_peer(d):
        return {"col": at(u, d) * n + x}

    def x_peer(d):
        return {"col": u * n + at(x, d)}

    barrier = pltpu.get_barrier_semaphore()
    peers = [dp_peer] + [f(d) for f in (z_peer, y_peer, u_peer, x_peer) for d in others]
    for peer in peers:
        pl.semaphore_signal(
            barrier, inc=1, device_id=peer, device_id_type=pl.DeviceIdType.MESH
        )

    issued = []

    def when(cond, body):
        if cond is None:
            body()
        else:
            pl.when(cond)(body)

    def send(src, dst, landed, peer, sends=None, receives=None):
        index = len(issued)

        def describe(source, target):
            return pltpu.make_async_remote_copy(
                src_ref=source,
                dst_ref=target,
                send_sem=send_sems.at[index],
                recv_sem=recv_sems.at[index],
                device_id=peer,
                device_id_type=pl.DeviceIdType.MESH,
            )

        when(sends, lambda: describe(src, dst).start())
        issued.append(lambda: when(sends, lambda: describe(src, dst).wait_send()))
        return lambda: when(receives, lambda: describe(landed, landed).wait_recv())

    def wait(handles):
        for handle in handles:
            handle()

    def block(i):
        return pl.ds(pl.multiple_of(i * rows, rows), rows)

    def group(i):
        return pl.ds(pl.multiple_of(i * chunk, chunk), chunk)

    def gather_z(view):
        return [
            send(view(row), view(row), view(y * n + at(z, -d)), z_peer(d))
            for d in others
        ]

    def gather_y(view, up):
        handles = []
        for d in others:
            target, source = (y + d, y - d) if up else (y - d, y + d)
            sends = target < n if up else target >= 0
            receives = source >= 0 if up else source < n
            handles.append(
                send(
                    view(y),
                    view(y),
                    view(at(y, -d if up else d)),
                    y_peer(d if up else -d),
                    sends,
                    receives,
                )
            )
        return handles

    kf[block(row), :] = k_ref[...]
    vf[block(row), :] = v_ref[...]
    qf[block(row), :] = q_ref[...]
    half = cols // 2
    mine = pl.ds(pl.multiple_of(dp * half, half), half)
    theirs = pl.ds(pl.multiple_of((1 - dp) * half, half), half)
    wf[row, mine, :] = wt_ref[mine, :]
    pl.semaphore_wait(barrier, len(peers))

    def w_view(i):
        return wf.at[i, mine, :]

    def w_group(i, part=mine):
        return wf.at[pl.ds(i * n, n), part, :]

    k_z = gather_z(lambda i: kf.at[block(i), :])
    v_z = gather_z(lambda i: vf.at[block(i), :])
    w_z = gather_z(w_view)
    wait(k_z)
    k_y = gather_y(lambda i: kf.at[group(i), :], True)
    wait(v_z)
    v_y = gather_y(lambda i: vf.at[group(i), :], True)
    wait(w_z)
    w_y = [
        send(w_group(y), w_group(y), w_group(at(y, -d)), y_peer(d)) for d in others
    ]
    w_d = [send(w_group(y), w_group(y), w_group(y, theirs), dp_peer)]
    q_z = gather_z(lambda i: qf.at[block(i), :])

    heads = [slice(h * HEAD, (h + 1) * HEAD) for h in range(2)]
    query_pos = row * rows + lax.broadcasted_iota(jnp.int32, (rows, chunk), 0)
    key_pos = lax.broadcasted_iota(jnp.int32, (rows, chunk), 1)

    def forward(j, carry):
        visible = key_pos + j * chunk <= query_pos
        result = []
        for lanes, (top, total, acc) in zip(heads, carry):
            scores = dot_nt(q_ref[:, lanes], kf[group(j), lanes]) * SCALE
            scores = jnp.where(visible, scores, NEG)
            new_top = jnp.maximum(top, jnp.max(scores, axis=1, keepdims=True))
            weights = jnp.exp(scores - new_top)
            fade = jnp.exp(top - new_top)
            total = fade * total + jnp.sum(weights, axis=1, keepdims=True)
            acc = fade * acc + dot(weights.astype(BF16), vf[group(j), lanes])
            result.append((new_top, total, acc))
        return tuple(result)

    wait(k_y)
    wait(v_y)
    start = tuple(
        (
            jnp.full((rows, 1), NEG, F32),
            jnp.zeros((rows, 1), F32),
            jnp.zeros((rows, HEAD), F32),
        )
        for _ in heads
    )
    done = lax.fori_loop(0, y + 1, forward, start)
    log_norms = []
    own_of = x * n + u
    for lanes, (top, total, acc) in zip(heads, done):
        of[own_of, :, lanes] = (acc / total).astype(BF16)
        log_norms.append(top + jnp.log(total))

    o_u = [
        send(of.at[own_of], of.at[own_of], of.at[x * n + at(u, -d)], u_peer(d))
        for d in far
    ]

    for d, handle in zip(others, w_y):
        handle()
        source = at(y, -d)
        w_d.append(send(w_group(source), w_group(source), w_group(source, theirs), dp_peer))
    wait(q_z)
    q_y = gather_y(lambda i: qf.at[group(i), :], False)
    wait(w_d)

    h_x = {}
    for d in far + [0]:
        for e in far + [0]:
            target_x, target_u = at(x, d), at(u, e)
            slot = target_x * n + target_u
            hs[slot] = dot(g_ref[...], wf[target_u * n + target_x]).astype(BF16)
            if d:
                h_x[d, e] = send(
                    hs.at[slot], hx.at[d - 1, e], hx.at[d - 1, e], x_peer(d)
                )

    wait(o_u)
    mine_x = pl.ds(x * n, n)
    o_x = [
        send(of.at[mine_x], of.at[mine_x], of.at[pl.ds(at(x, -d) * n, n)], x_peer(d))
        for d in far
    ]

    h_u = []
    for e in far + [0]:
        total = hs[x * n + at(u, e)].astype(F32)
        for d in far:
            h_x[d, e]()
            total = total + hx[d - 1, e].astype(F32)
        hz[e] = total.astype(BF16)
        if e:
            h_u.append(send(hz.at[e], hr.at[e - 1], hr.at[e - 1], u_peer(e)))

    wait(h_u)
    upstream = hz[0].astype(F32)
    for e in others:
        upstream = upstream + hr[e - 1].astype(F32)
    df[block(row), :] = upstream.astype(BF16)
    d_z = gather_z(lambda i: df.at[block(i), :])
    own_up = df[block(row), :].astype(F32)
    attended = of[own_of].astype(F32)
    dots = [
        jnp.sum(own_up[:, lanes] * attended[:, lanes], axis=1, keepdims=True)
        for lanes in heads
    ]
    lane = lax.broadcasted_iota(jnp.int32, (rows, rows), 1)
    table = jnp.zeros((rows, rows), F32)
    for i, column in enumerate(log_norms + dots):
        table = jnp.where(lane == i, column, table)
    st[:, block(row)] = jnp.transpose(table)[:8, :]
    s_z = gather_z(lambda i: st.at[:, block(i)])

    wait(o_x)

    def weight_part(which, target_y):
        first = (which * n * n + target_y * n) // 2
        for i in range(n // 2):
            c = first + i
            part = dot(gt_ref[...], of[lax.rem(c, n) * n + c // n]).astype(BF16)
            gp[2 * c] = part[:, :HEAD]
            gp[2 * c + 1] = part[:, HEAD:]

    g_d = {}
    for d in far + [0]:
        target_y = at(y, d)
        weight_part(1 - dp, target_y)
        away = pl.ds((1 - dp) * n * n + target_y * n, n)
        here = pl.ds(target_y * n, n)
        g_d[d] = send(gp.at[away], gd.at[here], gd.at[here], dp_peer)
    for d in far + [0]:
        weight_part(dp, at(y, d))

    wait(d_z)
    d_y = gather_y(lambda i: df.at[group(i), :], False)
    wait(s_z)
    s_y = gather_y(lambda i: st.at[:, group(i)], False)

    g_y = []
    for d in far + [0]:
        target_y = at(y, d)
        g_d[d]()
        for i in range(n):
            slot = target_y * n + i
            gy[slot] = (
                gp[dp * n * n + slot].astype(F32) + gd[slot].astype(F32)
            ).astype(BF16)
        if d:
            here = pl.ds(target_y * n, n)
            g_y.append(send(gy.at[here], gyr.at[d - 1], gyr.at[d - 1], y_peer(d)))

    def queries_pass(j, carry):
        visible = key_pos + j * chunk <= query_pos
        result = []
        for h, lanes in enumerate(heads):
            keys = kf[group(j), lanes]
            scores = dot_nt(q_ref[:, lanes], keys) * SCALE
            probs = jnp.where(visible, jnp.exp(scores - log_norms[h]), 0.0)
            slopes = dot_nt(df[block(row), lanes], vf[group(j), lanes])
            slopes = (probs * (slopes - dots[h])).astype(BF16)
            result.append(carry[h] + dot(slopes, keys))
        return tuple(result)

    zero = jnp.zeros((rows, HEAD), F32)
    sums = lax.fori_loop(0, y + 1, queries_pass, (zero, zero))
    for lanes, value in zip(heads, sums):
        dq_ref[:, lanes] = (value * SCALE).astype(BF16)

    def project(c, acc):
        return acc + dot_nt(of[lax.rem(c, n) * n + c // n], wf[c])

    out_ref[...] = lax.fori_loop(
        0, n * n, project, jnp.zeros((rows, cols), F32)
    ).astype(BF16)

    wait(g_y)
    g_z = []
    for d in others + [0]:
        target_z = at(z, d)
        total = gy[y * n + target_z].astype(F32)
        for e in others:
            total = total + gyr[e - 1, target_z].astype(F32)
        gz[d] = total.astype(BF16)
        if d:
            g_z.append(send(gz.at[d], gzr.at[d - 1], gzr.at[d - 1], z_peer(d)))

    wait(q_y)
    wait(d_y)
    wait(s_y)
    own_key = row * rows + lax.broadcasted_iota(jnp.int32, (rows, chunk), 0)

    def keys_pass(j, carry):
        visible = key_pos + j * chunk >= own_key
        result = []
        for h, lanes in enumerate(heads):
            queries = qf[group(j), lanes]
            ups = df[group(j), lanes]
            norm = st[h : h + 1, group(j)]
            away = st[2 + h : 3 + h, group(j)]
            scores = dot_nt(k_ref[:, lanes], queries) * SCALE
            probs = jnp.where(visible, jnp.exp(scores - norm), 0.0)
            slopes = dot_nt(v_ref[:, lanes], ups)
            slopes = (probs * (slopes - away)).astype(BF16)
            sum_k, sum_v = carry[h]
            result.append(
                (sum_k + dot(slopes, queries), sum_v + dot(probs.astype(BF16), ups))
            )
        return tuple(result)

    sums = lax.fori_loop(y, n, keys_pass, ((zero, zero), (zero, zero)))
    for lanes, (sum_k, sum_v) in zip(heads, sums):
        dk_ref[:, lanes] = (sum_k * SCALE).astype(BF16)
        dv_ref[:, lanes] = sum_v.astype(BF16)

    wait(g_z)
    total = gz[0].astype(F32)
    for d in others:
        total = total + gzr[d - 1].astype(F32)
    gw_ref[...] = total

    for finish in issued:
        finish()


def shards(n, queries, key_vectors, value_vectors, out_weight, out_grad):
    rows, width = queries.shape[1:]
    cols = out_grad.shape[2]
    blocks = n * n
    copies = (17 + n) * (n - 1) + 2 * n
    vmem = pl.BlockSpec(memory_space=pltpu.VMEM)
    full = pltpu.VMEM((blocks * rows, width), BF16)
    result = pl.pallas_call(
        functools.partial(kernel, n, rows, cols),
        out_shape=(
            jax.ShapeDtypeStruct((rows, cols), BF16),
            jax.ShapeDtypeStruct((rows, width), BF16),
            jax.ShapeDtypeStruct((rows, width), BF16),
            jax.ShapeDtypeStruct((rows, width), BF16),
            jax.ShapeDtypeStruct((cols, HEAD), F32),
        ),
        in_specs=[vmem] * 6,
        out_specs=(vmem,) * 5,
        scratch_shapes=[
            full,
            full,
            full,
            full,
            pltpu.VMEM((8, blocks * rows), F32),
            pltpu.VMEM((blocks, cols, width), BF16),
            pltpu.VMEM((blocks, rows, width), BF16),
            pltpu.VMEM((n - 1, n, rows, width), BF16),
            pltpu.VMEM((n, rows, width), BF16),
            pltpu.VMEM((n - 1, rows, width), BF16),
            pltpu.VMEM((blocks, rows, width), BF16),
            pltpu.VMEM((2 * blocks, cols, HEAD), BF16),
            pltpu.VMEM((blocks, cols, HEAD), BF16),
            pltpu.VMEM((blocks, cols, HEAD), BF16),
            pltpu.VMEM((n - 1, n, cols, HEAD), BF16),
            pltpu.VMEM((n, cols, HEAD), BF16),
            pltpu.VMEM((n - 1, cols, HEAD), BF16),
            pltpu.SemaphoreType.DMA((copies,)),
            pltpu.SemaphoreType.DMA((copies,)),
        ],
        compiler_params=pltpu.CompilerParams(
            collective_id=0, has_side_effects=True, vmem_limit_bytes=48 << 20
        ),
    )(
        queries[0],
        key_vectors[0],
        value_vectors[0],
        out_weight.T,
        out_grad[0],
        out_grad[0].T,
    )
    output, grad_queries, grad_keys, grad_values, grad_weight = result
    return (
        output[None],
        grad_queries[None],
        grad_keys[None],
        grad_values[None],
        grad_weight.T,
    )


def solution(mesh):
    n = math.isqrt(mesh.shape["row"])
    return jax.shard_map(
        functools.partial(shards, n),
        mesh=mesh,
        in_specs=(
            P("dp", "row", "col"),
            P("dp", "row", "col"),
            P("dp", "row", "col"),
            P("row", "col"),
            P("dp", "row", "col"),
        ),
        out_specs=(
            P("dp", "row", "col"),
            P("dp", "row", "col"),
            P("dp", "row", "col"),
            P("dp", "row", "col"),
            P(("dp", "row"), "col"),
        ),
        check_vma=False,
    )
```

time: 795 us -> 124 us (0.16)
  waiting for transfers between devices: 674 us -> 0 us
  Pallas kernels: 0 us -> 116 us
  blocking collectives: 68.5 us -> 0 us
  matrix products: 23.2 us -> 0 us
  between operations: 14.3 us -> 0.69 us
    all_gather x6 -> x0, waiting for transfers between devices: 381 us -> none  [the longest x1 85 us: shards(): lax.all_gather(value_vectors[0], 'row', axis=0, tiled=True)]
    reduce_scatter x2 -> x0, waiting for transfers between devices: 291 us -> none  [the longest x1 169 us: shards(): lax.psum_scatter(lax.dot_general(columns, grad_local, (((0,), (0,)), ((),...]
    pallas_call x0 -> x1, Pallas kernels: none -> 116 us  [shards(): pl.pallas_call(functools.partial(kernel, n, rows, cols), out_shape=(jax.S...]
    all_gather x2 -> x0, blocking collectives: 68.5 us -> none  [the longest x1 35.5 us: shards(): lax.all_gather(sent[3], 'row', axis=0, tiled=True)]
    dot_general x9 -> x0, matrix products: 23.2 us -> none  [the longest x2 5.44 us: causal_scores(): jnp.einsum('qhe,khe->qhk', query_part, key_part, preferred_element_type=j...]
  transfers between devices with their start and end apart: 8 -> 0, of which waited for: 8 -> 0; matrix products, arithmetic and copies ran while one was open for 4% -> 0% of each run, Pallas kernels for 0% -> 0%
where the time goes in v1:
time: 124 us
  Pallas kernels  116 us (94%)
  local copies, waits for them, and re-layouts  6.78 us (5%)
    pallas_call x1, Pallas kernels, shards(): pl.pallas_call(functools.partial(kernel, n, rows, cols), out_shape=(jax.S...  116 us
    unnamed x15, local copies, waits for them, and re-layouts  5.82 us

profile of v1, /device:TPU:1, one launch (start us, length us, event | category | flops | bytes accessed | tf_op | source)
XLA Modules:
  0.0 123.5 jit_solution(7792303983295560821)
XLA Ops:
  0.6 0.0 copy-start.2
  0.6 0.0 copy-start
  0.7 1.0 copy.10.g_ref
  1.6 0.0 copy-done.2
  1.6 0.0 copy-done
  1.6 0.0 copy-start.1
  1.6 0.9 copy-done.1
  2.5 0.0 copy-start.3
  2.5 0.8 copy-done.3
  3.4 0.0 copy-start.4
  3.4 0.8 copy-done.4
  4.2 116.1 %shard_map.92 = (bf16[128,192]{1,0:T(8,128)(2,1)S(1)}, bf16[128,256]{1,0:T(8,128)(2,1)S(1)}, bf16[128,256]{1,0:T(8,128)(2,1)S(1)}, bf16[128,256]{1,0:T(8,128)(2,1)S(1)}, f32[192,128]{1,0:T(8,128)S(1)}) custom-call(bf16[128,256]{1,0:T(8,128)(2,1)S(1)} %bitcast.16, bf16[128,256]{1,0:T(8,128)(2,1)S(1)} %bitcast.17, bf16[128,256]{1,0:T(8,128)(2,1)S(1)} %bitcast.18, ...), custom_call_target="tpu_custom_call" | custom-call | tf_op jit(solution)/shard_map/pallas_call | solution.py:394
  120.3 0.7 copy.11
  121.0 0.6 copy.16
  121.6 0.6 copy.17
  122.3 0.6 copy.18
  122.9 0.6 copy.19
Async XLA Ops:
  0.6 1.0 copy-start.2
  0.6 1.0 copy-start
  1.6 0.9 copy-start.1
  2.5 0.8 copy-start.3
  3.4 0.8 copy-start.4

commit v2 on v1

v2 whole, which is shorter than its diff:
```python
import functools
import math

import jax
import jax.numpy as jnp
from jax import lax
from jax.experimental import pallas as pl
from jax.experimental.pallas import tpu as pltpu
from jax.sharding import PartitionSpec as P

HEAD = 128
NEG = -1e30
SCALE = 1.0 / math.sqrt(HEAD)
F32 = jnp.float32
BF16 = jnp.bfloat16
NT = (((1,), (1,)), ((), ()))
TN = (((0,), (0,)), ((), ()))


def dot(a, b):
    return jnp.dot(a, b, preferred_element_type=F32)


def dot_nt(a, b):
    return lax.dot_general(a, b, NT, preferred_element_type=F32)


def flip(a):
    size = a.shape[0]
    eye = (
        lax.broadcasted_iota(jnp.int32, (size, size), 0)
        == lax.broadcasted_iota(jnp.int32, (size, size), 1)
    )
    eye = jnp.where(eye, 1.0, 0.0).astype(BF16)
    return lax.dot_general(a, eye, TN, preferred_element_type=F32).astype(BF16)


def kernel(
    n,
    rows,
    cols,
    q_hbm,
    k_hbm,
    v_hbm,
    w_hbm,
    g_hbm,
    out_ref,
    dq_ref,
    dk_ref,
    dv_ref,
    gw_ref,
    q_in,
    k_in,
    v_in,
    w_in,
    qs,
    ks,
    vs,
    ws,
    kf,
    vf,
    qf,
    df,
    st,
    wf,
    gf,
    gt,
    hs,
    hx,
    hz,
    hr,
    of,
    top_ref,
    sum_ref,
    acc_ref,
    gp,
    gd,
    gy,
    gyr,
    gz,
    gzr,
    ox,
    oxr,
    dx,
    dxr,
    load_sems,
    send_sems,
    recv_sems,
):
    dp, row, col = lax.axis_index("dp"), lax.axis_index("row"), lax.axis_index("col")
    m = n // 2
    y, z = row // n, lax.rem(row, n)
    zh, side = z // 2, lax.rem(z, 2)
    u, x = col // n, lax.rem(col, n)
    pair = y * m + zh
    span = 2 * rows
    chunk = n * rows
    others = list(range(1, n))
    far = sorted(others, key=lambda d: -min(d, n - d))
    near = far[::-1]

    def at(base, d):
        return lax.rem(base + d + n, n)

    dp_peer = {"dp": 1 - dp}
    twin = {"row": row + 1 - 2 * side}

    def z_peer(d):
        return {"row": y * n + at(z, d)}

    def h_peer(d):
        return {"row": y * n + 2 * lax.rem(zh + d, m) + side}

    def y_peer(d):
        return {"row": at(y, d) * n + z}

    def u_peer(d):
        return {"col": at(u, d) * n + x}

    def x_peer(d):
        return {"col": u * n + at(x, d)}

    def block(i):
        return pl.ds(pl.multiple_of(i * rows, rows), rows)

    def span_of(i):
        return pl.ds(pl.multiple_of(i * span, span), span)

    def group(i):
        return pl.ds(pl.multiple_of(i * chunk, chunk), chunk)

    loads = [
        pltpu.make_async_copy(source, target, load_sems.at[i])
        for i, (source, target) in enumerate(
            [
                (w_hbm, w_in),
                (g_hbm, gf.at[block(side), :]),
                (k_hbm, k_in),
                (q_hbm, q_in),
                (v_hbm, v_in),
            ]
        )
    ]
    for load in loads:
        load.start()

    barrier = pltpu.get_barrier_semaphore()
    peers = [dp_peer] + [f(d) for f in (z_peer, y_peer, u_peer, x_peer) for d in others]
    for peer in peers:
        pl.semaphore_signal(
            barrier, inc=1, device_id=peer, device_id_type=pl.DeviceIdType.MESH
        )

    issued = []

    def when(cond, body):
        if cond is None:
            body()
        else:
            pl.when(cond)(body)

    def send(src, dst, landed, peer, sends=None, receives=None):
        index = len(issued)

        def describe(source, target):
            return pltpu.make_async_remote_copy(
                src_ref=source,
                dst_ref=target,
                send_sem=send_sems.at[index],
                recv_sem=recv_sems.at[index],
                device_id=peer,
                device_id_type=pl.DeviceIdType.MESH,
            )

        when(sends, lambda: describe(src, dst).start())
        issued.append(lambda: when(sends, lambda: describe(src, dst).wait_send()))
        return lambda inside=False: when(
            None if inside else receives, lambda: describe(landed, landed).wait_recv()
        )

    def wait(handles):
        for handle in handles:
            handle()

    half = cols // 2
    mine = pl.ds(pl.multiple_of(dp * half, half), half)
    theirs = pl.ds(pl.multiple_of((1 - dp) * half, half), half)
    lanes = [slice(h * HEAD, (h + 1) * HEAD) for h in range(2)]

    for load in loads:
        load.wait()
    for h in range(2):
        ws[h] = flip(w_in[lanes[h], :])
    wf[row, mine, :] = ws[side, mine, :]
    for source, split, full in ((k_in, ks, kf), (q_in, qs, qf), (v_in, vs, vf)):
        for h in range(2):
            split[h] = source[:, lanes[h]]
        full[block(row), :] = split[side]
    pl.semaphore_wait(barrier, len(peers))

    def spread_z(split, full, d):
        source = y * n + at(z, -d)
        return send(
            split.at[lax.rem(at(z, d), 2)],
            full.at[block(row), :],
            full.at[block(source), :],
            z_peer(d),
        )

    def gather_h(view):
        return [
            send(view(pair), view(pair), view(y * m + lax.rem(zh + m - d, m)), h_peer(d))
            for d in range(1, m)
        ]

    def gather_y(view, up):
        handles = {}
        for d in near:
            target, source = (y + d, y - d) if up else (y - d, y + d)
            sends = target < n if up else target >= 0
            receives = source >= 0 if up else source < n
            handles[d] = send(
                view(y),
                view(y),
                view(at(y, -d if up else d)),
                y_peer(d if up else -d),
                sends,
                receives,
            )
        return handles

    def w_group(i, part=mine):
        return wf.at[pl.ds(i * n, n), part, :]

    w_z = [
        send(
            ws.at[lax.rem(at(z, d), 2), mine, :],
            wf.at[row, mine, :],
            wf.at[y * n + at(z, -d), mine, :],
            z_peer(d),
        )
        for d in others
    ]
    g_s = send(
        gf.at[block(side), :], gf.at[block(side), :], gf.at[block(1 - side), :], twin
    )
    k_z = [spread_z(ks, kf, d) for d in others]
    q_s = send(
        qs.at[1 - side],
        qf.at[block(row), :],
        qf.at[block(row + 1 - 2 * side), :],
        twin,
    )
    v_z = [spread_z(vs, vf, d) for d in others]

    wait(w_z)
    w_y = {
        d: send(w_group(y), w_group(y), w_group(at(y, -d)), y_peer(d)) for d in near
    }
    w_d = [send(w_group(y), w_group(y), w_group(y, theirs), dp_peer)]
    wait(k_z)
    k_y = gather_y(lambda i: kf.at[group(i), :], True)
    wait(v_z)
    v_y = gather_y(lambda i: vf.at[group(i), :], True)
    g_s()
    gt[:, : rows] = flip(gf[:rows, :])
    gt[:, rows:] = flip(gf[rows:, :])
    q_s()

    query_pos = pair * span + lax.broadcasted_iota(jnp.int32, (span, chunk), 0)
    key_pos = y * chunk + lax.broadcasted_iota(jnp.int32, (span, chunk), 1)

    def forward(j, first):
        scores = dot_nt(qf[span_of(pair), :], kf[group(j), :]) * SCALE
        if first:
            scores = jnp.where(key_pos <= query_pos, scores, NEG)
        new_top = jnp.max(scores, axis=1, keepdims=True)
        if not first:
            top = top_ref[:, :1]
            new_top = jnp.maximum(top, new_top)
        weights = jnp.exp(scores - new_top)
        total = jnp.sum(weights, axis=1, keepdims=True)
        acc = dot(weights.astype(BF16), vf[group(j), :])
        if not first:
            fade = jnp.exp(top - new_top)
            total = fade * sum_ref[:, :1] + total
            acc = fade * acc_ref[...] + acc
        top_ref[...] = jnp.broadcast_to(new_top, top_ref.shape)
        sum_ref[...] = jnp.broadcast_to(total, sum_ref.shape)
        acc_ref[...] = acc

    forward(y, True)
    for d in near:
        w_y[d]()
        source = at(y, -d)
        w_d.append(
            send(w_group(source), w_group(source), w_group(source, theirs), dp_peer)
        )
    q_z = [
        send(
            qs.at[lax.rem(at(z, d), 2)],
            qf.at[block(row), :],
            qf.at[block(y * n + at(z, -d)), :],
            z_peer(d),
            at(z, d) != z + 1 - 2 * side,
            at(z, -d) != z + 1 - 2 * side,
        )
        for d in others
    ]
    wait(w_d)

    h_x = {}
    for d in far + [0]:
        for e in far + [0]:
            target_x, target_u = at(x, d), at(u, e)
            slot = target_x * n + target_u
            hs[slot] = dot(gf[...], wf[target_u * n + target_x]).astype(BF16)
            if d:
                h_x[d, e] = send(
                    hs.at[slot], hx.at[d - 1, e], hx.at[d - 1, e], x_peer(d)
                )

    for d in near:

        @pl.when(y >= d)
        def _(d=d):
            k_y[d](True)
            v_y[d](True)
            forward(y - d, False)

    own_of = x * n + u
    total = sum_ref[:, :1]
    of[own_of] = (acc_ref[...] / total).astype(BF16)
    log_norm = top_ref[:, :1] + jnp.log(total)
    o_u = {
        d: send(of.at[own_of], of.at[own_of], of.at[x * n + at(u, -d)], u_peer(d))
        for d in far
    }

    def spread_x(e):
        return [
            send(
                of.at[x * n + at(u, -e)],
                of.at[x * n + at(u, -e)],
                of.at[at(x, -d) * n + at(u, -e)],
                x_peer(d),
            )
            for d in far
        ]

    o_x = spread_x(0)
    wait(q_z)
    q_y = gather_y(lambda i: qf.at[group(i), :], False)

    h_u = []
    for e in far + [0]:
        total = hs[x * n + at(u, e)].astype(F32)
        for d in far:
            h_x[d, e]()
            total = total + hx[d - 1, e].astype(F32)
        hz[e] = total.astype(BF16)
        if e:
            h_u.append(send(hz.at[e], hr.at[e - 1], hr.at[e - 1], u_peer(e)))

    for d in near:
        o_u[d]()
        o_x += spread_x(d)

    wait(h_u)
    upstream = hz[0].astype(F32)
    for e in others:
        upstream = upstream + hr[e - 1].astype(F32)
    df[span_of(pair), :] = upstream.astype(BF16)
    d_h = gather_h(lambda i: df.at[span_of(i), :])
    attended = of[own_of].astype(F32)
    row_dot = jnp.sum(
        df[span_of(pair), :].astype(F32) * attended, axis=1, keepdims=True
    )
    lane = lax.broadcasted_iota(jnp.int32, (span, HEAD), 1)
    table = jnp.where(lane == 0, log_norm, jnp.where(lane == 1, row_dot, 0.0))
    st[:, span_of(pair)] = jnp.transpose(table)[:8, :]
    s_h = gather_h(lambda i: st.at[:, span_of(i)])

    wait(d_h)
    d_y = gather_y(lambda i: df.at[group(i), :], False)
    wait(s_h)
    s_y = gather_y(lambda i: st.at[:, group(i)], False)

    wait(o_x)

    def weight_part(which, target_y):
        first = which * n * m + target_y * m
        for i in range(m):
            c = first + i
            part = dot(gt[...], of[lax.rem(c, n) * n + c // n])
            gp[c] = part.astype(BF16)

    g_d = {}
    for d in far + [0]:
        target_y = at(y, d)
        weight_part(1 - dp, target_y)
        away = pl.ds((1 - dp) * n * m + target_y * m, m)
        here = pl.ds(target_y * m, m)
        g_d[d] = send(gp.at[away], gd.at[here], gd.at[here], dp_peer)
    for d in far + [0]:
        weight_part(dp, at(y, d))

    g_y = []
    for d in far + [0]:
        target_y = at(y, d)
        g_d[d]()
        for i in range(m):
            slot = target_y * m + i
            gy[slot] = (
                gp[dp * n * m + slot].astype(F32) + gd[slot].astype(F32)
            ).astype(BF16)
        if d:
            here = pl.ds(target_y * m, m)
            g_y.append(send(gy.at[here], gyr.at[d - 1], gyr.at[d - 1], y_peer(d)))

    def project(c, acc):
        return acc + dot_nt(wf[c], of[lax.rem(c, n) * n + c // n])

    projected = lax.fori_loop(0, n * n, project, jnp.zeros((cols, span), F32))
    for h in range(2):
        ox[h] = projected[:, lanes[h]].astype(BF16)
    o_s = send(ox.at[1 - side], oxr, oxr, twin)

    def queries_pass(j, first, acc):
        keys = kf[group(j), :]
        scores = dot_nt(qf[span_of(pair), :], keys) * SCALE
        probs = jnp.exp(scores - log_norm)
        if first:
            probs = jnp.where(key_pos <= query_pos, probs, 0.0)
        slopes = dot_nt(df[span_of(pair), :], vf[group(j), :])
        slopes = (probs * (slopes - row_dot)).astype(BF16)
        return acc + dot(slopes, keys)

    acc = queries_pass(y, True, jnp.zeros((span, HEAD), F32))
    acc = lax.fori_loop(0, y, lambda j, acc: queries_pass(j, False, acc), acc)
    acc = (acc * SCALE).astype(BF16)
    dx[0, 0], dx[0, 1] = acc[:rows], acc[rows:]
    swaps = [send(dx.at[0, 1 - side], dxr.at[0], dxr.at[0], twin)]

    wait(g_y)
    g_z = []
    for d in list(range(1, m)) + [0]:
        target = lax.rem(zh + d, m)
        total = gy[y * m + target].astype(F32)
        for e in others:
            total = total + gyr[e - 1, target].astype(F32)
        gz[d] = total.astype(BF16)
        if d:
            g_z.append(send(gz.at[d], gzr.at[d - 1], gzr.at[d - 1], h_peer(d)))

    own_key = pair * span + lax.broadcasted_iota(jnp.int32, (span, chunk), 0)
    ask_pos = y * chunk + lax.broadcasted_iota(jnp.int32, (span, chunk), 1)

    def keys_pass(j, first):
        queries = qf[group(j), :]
        ups = df[group(j), :]
        norm = st[0:1, group(j)]
        away = st[1:2, group(j)]
        scores = dot_nt(kf[span_of(pair), :], queries) * SCALE
        probs = jnp.exp(scores - norm)
        if first:
            probs = jnp.where(ask_pos >= own_key, probs, 0.0)
        slopes = dot_nt(vf[span_of(pair), :], ups)
        slopes = (probs * (slopes - away)).astype(BF16)
        sum_k, sum_v = dot(slopes, queries), dot(probs.astype(BF16), ups)
        if first:
            acc_ref[...], sum_ref[...] = sum_k, sum_v
        else:
            acc_ref[...] += sum_k
            sum_ref[...] += sum_v

    keys_pass(y, True)
    for d in near:

        @pl.when(y + d < n)
        def _(d=d):
            q_y[d](True)
            d_y[d](True)
            s_y[d](True)
            keys_pass(y + d, False)

    for i, value in ((1, acc_ref[...] * SCALE), (2, sum_ref[...])):
        value = value.astype(BF16)
        dx[i, 0], dx[i, 1] = value[:rows], value[rows:]
        swaps.append(send(dx.at[i, 1 - side], dxr.at[i], dxr.at[i], twin))

    wait(g_z)
    total = gz[0].astype(F32)
    for d in range(1, m):
        total = total + gzr[d - 1].astype(F32)
    gw_ref[...] = total
    o_s()
    out_ref[...] = (ox[side].astype(F32) + oxr[...].astype(F32)).astype(BF16)
    for i, target in enumerate((dq_ref, dk_ref, dv_ref)):
        swaps[i]()
        own, other = dx[i, side], dxr[i]
        for h in range(2):
            target[:, lanes[h]] = jnp.where(side == h, own, other)

    for finish in issued:
        finish()


def shards(n, queries, key_vectors, value_vectors, out_weight, out_grad):
    rows, width = queries.shape[1:]
    cols = out_grad.shape[2]
    blocks, m = n * n, n // 2
    copies = 27 * (n - 1) + n * (n - 1) + 2 * n + 8 * m + 16
    vmem = pl.BlockSpec(memory_space=pltpu.VMEM)

    def buffer(*shape, kind=BF16):
        return pltpu.VMEM(shape, kind)

    full = buffer(blocks * rows, HEAD)
    span = 2 * rows
    result = pl.pallas_call(
        functools.partial(kernel, n, rows, cols),
        out_shape=(
            jax.ShapeDtypeStruct((cols, rows), BF16),
            jax.ShapeDtypeStruct((rows, width), BF16),
            jax.ShapeDtypeStruct((rows, width), BF16),
            jax.ShapeDtypeStruct((rows, width), BF16),
            jax.ShapeDtypeStruct((cols, HEAD), F32),
        ),
        in_specs=[pl.BlockSpec(memory_space=pl.ANY)] * 5,
        out_specs=(vmem,) * 5,
        scratch_shapes=[
            buffer(rows, width),
            buffer(rows, width),
            buffer(rows, width),
            buffer(width, cols),
            buffer(2, rows, HEAD),
            buffer(2, rows, HEAD),
            buffer(2, rows, HEAD),
            buffer(2, cols, HEAD),
            full,
            full,
            full,
            full,
            buffer(8, blocks * rows, kind=F32),
            buffer(blocks, cols, HEAD),
            buffer(span, cols),
            buffer(cols, span),
            buffer(blocks, span, HEAD),
            buffer(n - 1, n, span, HEAD),
            buffer(n, span, HEAD),
            buffer(n - 1, span, HEAD),
            buffer(blocks, span, HEAD),
            buffer(span, HEAD, kind=F32),
            buffer(span, HEAD, kind=F32),
            buffer(span, HEAD, kind=F32),
            buffer(blocks, cols, HEAD),
            buffer(n * m, cols, HEAD),
            buffer(n * m, cols, HEAD),
            buffer(n - 1, m, cols, HEAD),
            buffer(m, cols, HEAD),
            buffer(max(m - 1, 1), cols, HEAD),
            buffer(2, cols, rows),
            buffer(cols, rows),
            buffer(3, 2, rows, HEAD),
            buffer(3, rows, HEAD),
            pltpu.SemaphoreType.DMA((5,)),
            pltpu.SemaphoreType.DMA((copies,)),
            pltpu.SemaphoreType.DMA((copies,)),
        ],
        compiler_params=pltpu.CompilerParams(
            collective_id=0, has_side_effects=True, vmem_limit_bytes=48 << 20
        ),
    )(queries[0], key_vectors[0], value_vectors[0], out_weight, out_grad[0])
    output, grad_queries, grad_keys, grad_values, grad_weight = result
    return (
        output.T[None],
        grad_queries[None],
        grad_keys[None],
        grad_values[None],
        grad_weight.T,
    )


def solution(mesh):
    n = math.isqrt(mesh.shape["row"])
    return jax.shard_map(
        functools.partial(shards, n),
        mesh=mesh,
        in_specs=(
            P("dp", "row", "col"),
            P("dp", "row", "col"),
            P("dp", "row", "col"),
            P("row", "col"),
            P("dp", "row", "col"),
        ),
        out_specs=(
            P("dp", "row", "col"),
            P("dp", "row", "col"),
            P("dp", "row", "col"),
            P("dp", "row", "col"),
            P(("dp", "row"), "col"),
        ),
        check_vma=False,
    )
```

time: 124 us -> 90.9 us (0.73)
  Pallas kernels: 116 us -> 84.7 us
  local copies, waits for them, and re-layouts: 6.78 us -> 4.96 us
    pallas_call x1, Pallas kernels: 116 us -> 84.7 us  [shards(): pl.pallas_call(functools.partial(kernel, n, rows, cols), out_shape=(jax.S...]
where the time goes in v2:
time: 90.9 us; the launch traced here: 90.4 us
  Pallas kernels  84.7 us (93%)
  local copies, waits for them, and re-layouts  4.96 us (5%)
    pallas_call x1, Pallas kernels, shards(): pl.pallas_call(functools.partial(kernel, n, rows, cols), out_shape=(jax.S...  84.7 us
    unnamed x15, local copies, waits for them, and re-layouts  4.96 us

profile of v2, /device:TPU:1, one launch (start us, length us, event | category | flops | bytes accessed | tf_op | source)
XLA Modules:
  0.0 90.4 jit_solution(13697804080015153684)
XLA Ops:
  0.6 0.0 copy-start.3
  0.6 0.9 %copy.10 = bf16[1,128,192]{2,1,0:T(8,128)(2,1)S(1)} copy(bf16[1,128,192]{1,2,0:T(8,128)(2,1)} %param.9) | data formatting | bytes 98304 | tf_op args[4]
  1.6 0.0 copy-done.3
  1.6 0.0 copy-start
  1.6 0.0 copy-start.1
  1.6 0.0 copy-start.2
  1.6 0.1 copy.11.w_hbm
  1.7 0.7 copy-done
  2.4 0.0 copy-done.1
  2.5 0.0 copy-done.2
  2.5 84.7 %shard_map.92 = (bf16[192,128]{1,0:T(8,128)(2,1)S(1)}, bf16[128,256]{1,0:T(8,128)(2,1)S(1)}, bf16[128,256]{1,0:T(8,128)(2,1)S(1)}, bf16[128,256]{1,0:T(8,128)(2,1)S(1)}, f32[192,128]{1,0:T(8,128)S(1)}) custom-call(bf16[128,256]{1,0:T(8,128)(2,1)S(1)} %bitcast.16, bf16[128,256]{1,0:T(8,128)(2,1)S(1)} %bitcast.17, bf16[128,256]{1,0:T(8,128)(2,1)S(1)} %bitcast.18, ...), custom_call_target="tpu_custom_call" | custom-call | tf_op jit(solution)/shard_map/pallas_call | solution.py:521
  87.2 0.6 copy.17
  87.9 0.6 copy.18
  88.5 0.6 copy.19
  89.1 0.6 copy.20
  89.8 0.6 copy.21
Async XLA Ops:
  0.6 0.9 %copy-start.3 = (bf16[256,192]{0,1:T(8,128)(2,1)S(1)}, bf16[256,192]{0,1:T(8,128)(2,1)}, u32[]{:S(2)}) copy-start(bf16[256,192]{0,1:T(8,128)(2,1)} %param.8) | copy-start | bytes 294916
  1.6 0.8 copy-start
  1.6 0.9 copy-start.1
  1.6 0.9 copy-start.2

commit v3 on v2

--- a/solution.py
+++ b/solution.py
@@ -49,10 +49,6 @@
     dk_ref,
     dv_ref,
     gw_ref,
-    q_in,
-    k_in,
-    v_in,
-    w_in,
     qs,
     ks,
     vs,
@@ -98,18 +94,22 @@
     others = list(range(1, n))
     far = sorted(others, key=lambda d: -min(d, n - d))
     near = far[::-1]
+    z_steps = [(h, t) for h in range(m) for t in (1, 0) if h or t]
 
     def at(base, d):
         return lax.rem(base + d + n, n)
 
+    def at_h(d):
+        return lax.rem(zh + d + m, m)
+
     dp_peer = {"dp": 1 - dp}
     twin = {"row": row + 1 - 2 * side}
 
-    def z_peer(d):
-        return {"row": y * n + at(z, d)}
+    def z_row(h, t):
+        return y * n + 2 * at_h(h) + (1 - side if t else side)
 
     def h_peer(d):
-        return {"row": y * n + 2 * lax.rem(zh + d, m) + side}
+        return {"row": z_row(d, 0)}
 
     def y_peer(d):
         return {"row": at(y, d) * n + z}
@@ -129,29 +129,37 @@
     def group(i):
         return pl.ds(pl.multiple_of(i * chunk, chunk), chunk)
 
+    half = cols // 2
+    mine = pl.ds(pl.multiple_of(dp * half, half), half)
+    theirs = pl.ds(pl.multiple_of((1 - dp) * half, half), half)
+    own_lanes = block(side)
+    other_lanes = block(1 - side)
+
+    pieces = [
+        (w_hbm.at[mine, own_lanes], wf.at[row, mine, :]),
+        (w_hbm.at[mine, other_lanes], ws.at[mine, :]),
+        (g_hbm, gt.at[:, own_lanes]),
+    ]
+    for source, split, full in ((k_hbm, ks, kf), (q_hbm, qs, qf), (v_hbm, vs, vf)):
+        pieces.append((source.at[:, own_lanes], full.at[block(row), :]))
+        pieces.append((source.at[:, other_lanes], split))
     loads = [
         pltpu.make_async_copy(source, target, load_sems.at[i])
-        for i, (source, target) in enumerate(
-            [
-                (w_hbm, w_in),
-                (g_hbm, gf.at[block(side), :]),
-                (k_hbm, k_in),
-                (q_hbm, q_in),
-                (v_hbm, v_in),
-            ]
-        )
+        for i, (source, target) in enumerate(pieces)
     ]
-    for load in loads:
-        load.start()
 
     barrier = pltpu.get_barrier_semaphore()
-    peers = [dp_peer] + [f(d) for f in (z_peer, y_peer, u_peer, x_peer) for d in others]
+    peers = [dp_peer] + [{"row": z_row(h, t)} for h, t in z_steps]
+    peers += [f(d) for f in (u_peer, y_peer, x_peer) for d in far]
     for peer in peers:
         pl.semaphore_signal(
             barrier, inc=1, device_id=peer, device_id_type=pl.DeviceIdType.MESH
         )
+    for load in loads:
+        load.start()
 
     issued = []
+    slots = [0]
 
     def when(cond, body):
         if cond is None:
@@ -159,113 +167,137 @@
         else:
             pl.when(cond)(body)
 
-    def send(src, dst, landed, peer, sends=None, receives=None):
-        index = len(issued)
-
-        def describe(source, target):
+    def take(count):
+        slots[0] += count
+        return slots[0] - count
+
+    def send(src, dst, landed, peer, sends=None, receives=None, index=None, hears=None):
+        index = take(1) if index is None else index
+        hears = index if hears is None else hears
+
+        def describe(source, target, which):
             return pltpu.make_async_remote_copy(
                 src_ref=source,
                 dst_ref=target,
-                send_sem=send_sems.at[index],
-                recv_sem=recv_sems.at[index],
+                send_sem=send_sems.at[which],
+                recv_sem=recv_sems.at[which],
                 device_id=peer,
                 device_id_type=pl.DeviceIdType.MESH,
             )
 
-        when(sends, lambda: describe(src, dst).start())
-        issued.append(lambda: when(sends, lambda: describe(src, dst).wait_send()))
+        when(sends, lambda: describe(src, dst, index).start())
+        issued.append(
+            lambda: when(sends, lambda: describe(src, dst, index).wait_send())
+        )
         return lambda inside=False: when(
-            None if inside else receives, lambda: describe(landed, landed).wait_recv()
+            None if inside else receives,
+            lambda: describe(landed, landed, hears).wait_recv(),
         )
 
-    def wait(handles):
+    def wait(handles, *inside):
         for handle in handles:
-            handle()
-
-    half = cols // 2
-    mine = pl.ds(pl.multiple_of(dp * half, half), half)
-    theirs = pl.ds(pl.multiple_of((1 - dp) * half, half), half)
-    lanes = [slice(h * HEAD, (h + 1) * HEAD) for h in range(2)]
-
-    for load in loads:
-        load.wait()
-    for h in range(2):
-        ws[h] = flip(w_in[lanes[h], :])
-    wf[row, mine, :] = ws[side, mine, :]
-    for source, split, full in ((k_in, ks, kf), (q_in, qs, qf), (v_in, vs, vf)):
-        for h in range(2):
-            split[h] = source[:, lanes[h]]
-        full[block(row), :] = split[side]
-    pl.semaphore_wait(barrier, len(peers))
-
-    def spread_z(split, full, d):
-        source = y * n + at(z, -d)
-        return send(
-            split.at[lax.rem(at(z, d), 2)],
-            full.at[block(row), :],
-            full.at[block(source), :],
-            z_peer(d),
-        )
+            handle(*inside)
+
+    def spread_z(own, split, view, steps):
+        return {
+            (h, t): send(
+                split if t else own, view(row), view(z_row(-h, t)), {"row": z_row(h, t)}
+            )
+            for h, t in steps
+        }
 
     def gather_h(view):
         return [
-            send(view(pair), view(pair), view(y * m + lax.rem(zh + m - d, m)), h_peer(d))
+            send(view(pair), view(pair), view(y * m + at_h(-d)), h_peer(d))
             for d in range(1, m)
         ]
 
-    def gather_y(view, up):
+    def gather_y(view, h, up):
         handles = {}
         for d in near:
-            target, source = (y + d, y - d) if up else (y - d, y + d)
-            sends = target < n if up else target >= 0
-            receives = source >= 0 if up else source < n
+            if up is None:
+                sends = receives = None
+            elif up:
+                sends, receives = y + d < n, y >= d
+            else:
+                sends, receives = y >= d, y + d < n
+            s = -1 if up is False else 1
+            mid = at_h(-h)
             handles[d] = send(
-                view(y),
-                view(y),
-                view(at(y, -d if up else d)),
-                y_peer(d if up else -d),
+                view(y * m + mid),
+                view(y * m + mid),
+                view(at(y, -s * d) * m + mid),
+                y_peer(s * d),
                 sends,
                 receives,
             )
         return handles
 
+    def gather_full(arrived, view, up):
+        handles = []
+        for h in range(m):
+            wait([arrived[step] for step in z_steps if step[0] == h and step in arrived])
+            handles.append(gather_y(view, h, up))
+        return {d: [piece[d] for piece in handles] for d in near}
+
+    def k_view(i):
+        return kf.at[block(i), :]
+
+    def w_pair(i):
+        return wf.at[pl.ds(2 * i, 2), mine, :]
+
     def w_group(i, part=mine):
         return wf.at[pl.ds(i * n, n), part, :]
 
-    w_z = [
+    wait([load.wait for load in loads])
+    pl.semaphore_wait(barrier, len(peers))
+
+    w_z = spread_z(
+        wf.at[row, mine, :], ws.at[mine, :], lambda i: wf.at[i, mine, :], z_steps
+    )
+    g_s = send(gt.at[:, own_lanes], gt.at[:, own_lanes], gt.at[:, other_lanes], twin)
+    k_z = spread_z(kf.at[block(row), :], ks, lambda i: kf.at[block(i), :], z_steps)
+    q_s = spread_z(qf.at[block(row), :], qs, lambda i: qf.at[block(i), :], z_steps[:1])
+    v_z = spread_z(vf.at[block(row), :], vs, lambda i: vf.at[block(i), :], z_steps)
+
+    w_y = gather_full(w_z, w_pair, None)
+    w_d = {0: send(w_group(y), w_group(y), w_group(y, theirs), dp_peer)}
+    k_y = gather_full(k_z, lambda i: kf.at[span_of(i), :], True)
+    v_y = gather_full(v_z, lambda i: vf.at[span_of(i), :], True)
+    g_s()
+    gf[...] = flip(gt[...])
+
+    h_x = {}
+
+    def head_terms(d):
+        w_d[d]()
+        for e in far + [0]:
+            hs[d, e] = dot(gf[...], wf[at(y, d) * n + at(x, e)]).astype(BF16)
+            if e:
+                h_x[d, e] = send(
+                    hs.at[d, e], hx.at[d, e - 1], hx.at[d, e - 1], x_peer(e)
+                )
+
+    u_base = take(n)
+
+    def head_sums(d):
+        total = hs[d, 0].astype(F32)
+        for e in far:
+            h_x[d, e]()
+            total = total + hx[d, e - 1].astype(F32)
+        hz[d] = total.astype(BF16)
+        target = at(y, d)
+        e = lax.rem(target - u + n, n)
         send(
-            ws.at[lax.rem(at(z, d), 2), mine, :],
-            wf.at[row, mine, :],
-            wf.at[y * n + at(z, -d), mine, :],
-            z_peer(d),
+            hz.at[d],
+            hr.at[e],
+            hr.at[e],
+            {"col": target * n + x},
+            target != u,
+            index=u_base + e,
         )
-        for d in others
-    ]
-    g_s = send(
-        gf.at[block(side), :], gf.at[block(side), :], gf.at[block(1 - side), :], twin
-    )
-    k_z = [spread_z(ks, kf, d) for d in others]
-    q_s = send(
-        qs.at[1 - side],
-        qf.at[block(row), :],
-        qf.at[block(row + 1 - 2 * side), :],
-        twin,
-    )
-    v_z = [spread_z(vs, vf, d) for d in others]
-
-    wait(w_z)
-    w_y = {
-        d: send(w_group(y), w_group(y), w_group(at(y, -d)), y_peer(d)) for d in near
-    }
-    w_d = [send(w_group(y), w_group(y), w_group(y, theirs), dp_peer)]
-    wait(k_z)
-    k_y = gather_y(lambda i: kf.at[group(i), :], True)
-    wait(v_z)
-    v_y = gather_y(lambda i: vf.at[group(i), :], True)
-    g_s()
-    gt[:, : rows] = flip(gf[:rows, :])
-    gt[:, rows:] = flip(gf[rows:, :])
-    q_s()
+
+    head_terms(0)
 
     query_pos = pair * span + lax.broadcasted_iota(jnp.int32, (span, chunk), 0)
     key_pos = y * chunk + lax.broadcasted_iota(jnp.int32, (span, chunk), 1)
@@ -289,43 +321,23 @@
         sum_ref[...] = jnp.broadcast_to(total, sum_ref.shape)
         acc_ref[...] = acc
 
+    for d in near:
+        wait(w_y[d])
+        source = at(y, -d)
+        w_d[n - d] = send(w_group(source), w_group(source), w_group(source, theirs), dp_peer)
+    wait(q_s.values())
     forward(y, True)
     for d in near:
-        w_y[d]()
-        source = at(y, -d)
-        w_d.append(
-            send(w_group(source), w_group(source), w_group(source, theirs), dp_peer)
-        )
-    q_z = [
-        send(
-            qs.at[lax.rem(at(z, d), 2)],
-            qf.at[block(row), :],
-            qf.at[block(y * n + at(z, -d)), :],
-            z_peer(d),
-            at(z, d) != z + 1 - 2 * side,
-            at(z, -d) != z + 1 - 2 * side,
-        )
-        for d in others
-    ]
-    wait(w_d)
-
-    h_x = {}
-    for d in far + [0]:
-        for e in far + [0]:
-            target_x, target_u = at(x, d), at(u, e)
-            slot = target_x * n + target_u
-            hs[slot] = dot(gf[...], wf[target_u * n + target_x]).astype(BF16)
-            if d:
-                h_x[d, e] = send(
-                    hs.at[slot], hx.at[d - 1, e], hx.at[d - 1, e], x_peer(d)
-                )
+        head_terms(n - d)
+    q_z = spread_z(qf.at[block(row), :], qs, lambda i: qf.at[block(i), :], z_steps[1:])
+    head_sums(0)
 
     for d in near:
 
         @pl.when(y >= d)
         def _(d=d):
-            k_y[d](True)
-            v_y[d](True)
+            wait(k_y[d], True)
+            wait(v_y[d], True)
             forward(y - d, False)
 
     own_of = x * n + u
@@ -349,29 +361,29 @@
         ]
 
     o_x = spread_x(0)
-    wait(q_z)
-    q_y = gather_y(lambda i: qf.at[group(i), :], False)
-
-    h_u = []
-    for e in far + [0]:
-        total = hs[x * n + at(u, e)].astype(F32)
-        for d in far:
-            h_x[d, e]()
-            total = total + hx[d - 1, e].astype(F32)
-        hz[e] = total.astype(BF16)
-        if e:
-            h_u.append(send(hz.at[e], hr.at[e - 1], hr.at[e - 1], u_peer(e)))
+    for d in near:
+        head_sums(n - d)
+    q_y = gather_full(q_z, lambda i: qf.at[span_of(i), :], False)
 
     for d in near:
         o_u[d]()
         o_x += spread_x(d)
 
-    wait(h_u)
-    upstream = hz[0].astype(F32)
     for e in others:
-        upstream = upstream + hr[e - 1].astype(F32)
+        pltpu.make_async_remote_copy(
+            src_ref=hr.at[e],
+            dst_ref=hr.at[e],
+            send_sem=send_sems.at[u_base + e],
+            recv_sem=recv_sems.at[u_base + e],
+            device_id=u_peer(e),
+            device_id_type=pl.DeviceIdType.MESH,
+        ).wait_recv()
+    upstream = hz[lax.rem(u - y + n, n)].astype(F32)
+    for e in others:
+        upstream = upstream + hr[e].astype(F32)
     df[span_of(pair), :] = upstream.astype(BF16)
     d_h = gather_h(lambda i: df.at[span_of(i), :])
+    d_y = [gather_y(lambda i: df.at[span_of(i), :], 0, False)]
     attended = of[own_of].astype(F32)
     row_dot = jnp.sum(
         df[span_of(pair), :].astype(F32) * attended, axis=1, keepdims=True
@@ -380,11 +392,13 @@
     table = jnp.where(lane == 0, log_norm, jnp.where(lane == 1, row_dot, 0.0))
     st[:, span_of(pair)] = jnp.transpose(table)[:8, :]
     s_h = gather_h(lambda i: st.at[:, span_of(i)])
-
-    wait(d_h)
-    d_y = gather_y(lambda i: df.at[group(i), :], False)
-    wait(s_h)
-    s_y = gather_y(lambda i: st.at[:, group(i)], False)
+    s_y = [gather_y(lambda i: st.at[:, span_of(i)], 0, False)]
+
+    for h in range(1, m):
+        d_h[h - 1]()
+        d_y.append(gather_y(lambda i: df.at[span_of(i), :], h, False))
+        s_h[h - 1]()
+        s_y.append(gather_y(lambda i: st.at[:, span_of(i)], h, False))
 
     wait(o_x)
 
@@ -418,6 +432,8 @@
             here = pl.ds(target_y * m, m)
             g_y.append(send(gy.at[here], gyr.at[d - 1], gyr.at[d - 1], y_peer(d)))
 
+    lanes = [slice(h * HEAD, (h + 1) * HEAD) for h in range(2)]
+
     def project(c, acc):
         return acc + dot_nt(wf[c], of[lax.rem(c, n) * n + c // n])
 
@@ -445,7 +461,7 @@
     wait(g_y)
     g_z = []
     for d in list(range(1, m)) + [0]:
-        target = lax.rem(zh + d, m)
+        target = at_h(d)
         total = gy[y * m + target].astype(F32)
         for e in others:
             total = total + gyr[e - 1, target].astype(F32)
@@ -479,9 +495,10 @@
 
         @pl.when(y + d < n)
         def _(d=d):
-            q_y[d](True)
-            d_y[d](True)
-            s_y[d](True)
+            wait(q_y[d], True)
+            for h in range(m):
+                d_y[h][d](True)
+                s_y[h][d](True)
             keys_pass(y + d, False)
 
     for i, value in ((1, acc_ref[...] * SCALE), (2, sum_ref[...])):
@@ -506,11 +523,23 @@
         finish()
 
 
+def store_all(*refs):
+    count = len(refs) // 2
+    copies = [
+        pltpu.make_async_copy(refs[i], refs[count + i], refs[-1].at[i])
+        for i in range(count)
+    ]
+    for copy in copies:
+        copy.start()
+    for copy in copies:
+        copy.wait()
+
+
 def shards(n, queries, key_vectors, value_vectors, out_weight, out_grad):
     rows, width = queries.shape[1:]
     cols = out_grad.shape[2]
     blocks, m = n * n, n // 2
-    copies = 27 * (n - 1) + n * (n - 1) + 2 * n + 8 * m + 16
+    copies = 112
     vmem = pl.BlockSpec(memory_space=pltpu.VMEM)
 
     def buffer(*shape, kind=BF16):
@@ -527,17 +556,13 @@
             jax.ShapeDtypeStruct((rows, width), BF16),
             jax.ShapeDtypeStruct((cols, HEAD), F32),
         ),
-        in_specs=[pl.BlockSpec(memory_space=pl.ANY)] * 5,
+        in_specs=[pl.BlockSpec(memory_space=pltpu.HBM)] * 5,
         out_specs=(vmem,) * 5,
         scratch_shapes=[
-            buffer(rows, width),
-            buffer(rows, width),
-            buffer(rows, width),
-            buffer(width, cols),
-            buffer(2, rows, HEAD),
-            buffer(2, rows, HEAD),
-            buffer(2, rows, HEAD),
-            buffer(2, cols, HEAD),
+            buffer(rows, HEAD),
+            buffer(rows, HEAD),
+            buffer(rows, HEAD),
+            buffer(cols, HEAD),
             full,
             full,
             full,
@@ -546,10 +571,10 @@
             buffer(blocks, cols, HEAD),
             buffer(span, cols),
             buffer(cols, span),
-            buffer(blocks, span, HEAD),
-            buffer(n - 1, n, span, HEAD),
+            buffer(n, n, span, HEAD),
+            buffer(n, n - 1, span, HEAD),
             buffer(n, span, HEAD),
-            buffer(n - 1, span, HEAD),
+            buffer(n, span, HEAD),
             buffer(blocks, span, HEAD),
             buffer(span, HEAD, kind=F32),
             buffer(span, HEAD, kind=F32),
@@ -564,14 +589,21 @@
             buffer(cols, rows),
             buffer(3, 2, rows, HEAD),
             buffer(3, rows, HEAD),
-            pltpu.SemaphoreType.DMA((5,)),
+            pltpu.SemaphoreType.DMA((9,)),
             pltpu.SemaphoreType.DMA((copies,)),
             pltpu.SemaphoreType.DMA((copies,)),
         ],
         compiler_params=pltpu.CompilerParams(
             collective_id=0, has_side_effects=True, vmem_limit_bytes=48 << 20
         ),
-    )(queries[0], key_vectors[0], value_vectors[0], out_weight, out_grad[0])
+    )(queries[0], key_vectors[0], value_vectors[0], out_weight.T, out_grad[0].T)
+    result = pl.pallas_call(
+        store_all,
+        out_shape=[jax.ShapeDtypeStruct(a.shape, a.dtype) for a in result],
+        in_specs=[vmem] * 5,
+        out_specs=[pl.BlockSpec(memory_space=pltpu.HBM)] * 5,
+        scratch_shapes=[pltpu.SemaphoreType.DMA((5,))],
+    )(*result)
     output, grad_queries, grad_keys, grad_values, grad_weight = result
     return (
         output.T[None],

time: 90.9 us -> 95.7 us (1.053)
  Pallas kernels: 84.7 us -> 87.2 us
  local copies, waits for them, and re-layouts: 4.96 us -> 7.3 us
    unnamed x15 -> x20, local copies, waits for them, and re-layouts: 4.96 us -> 7.3 us
    pallas_call x0 -> x1, Pallas kernels: none -> 1.78 us  [shards(): pl.pallas_call(store_all, out_shape=[jax.ShapeDtypeStruct(a.shape, a.dtyp...]
where the time goes in v3:
time: 95.7 us; the launch traced here: 95.2 us
  Pallas kernels  87.2 us (91%)
  local copies, waits for them, and re-layouts  7.3 us (8%)
    pallas_call x1, Pallas kernels, shards(): pl.pallas_call(functools.partial(kernel, n, rows, cols), out_shape=(jax.S...  85.4 us
    unnamed x20, local copies, waits for them, and re-layouts  7.3 us

profile of v3, /device:TPU:1, one launch (start us, length us, event | category | flops | bytes accessed | tf_op | source)
XLA Modules:
  0.0 95.2 jit_solution(13907428493042270472)
XLA Ops:
  0.6 0.0 copy-start
  0.6 0.9 copy-done
  1.5 0.0 copy-start.2
  1.5 0.8 copy-done.2
  2.4 0.0 copy-start.3
  2.4 0.8 copy-done.3
  3.2 0.0 copy-start.4
  3.2 0.8 copy-done.4
  4.0 0.0 copy-start.8
  4.0 0.8 copy-done.8
  4.8 85.4 %shard_map.92 = (bf16[192,128]{1,0:T(8,128)(2,1)S(1)}, bf16[128,256]{1,0:T(8,128)(2,1)S(1)}, bf16[128,256]{1,0:T(8,128)(2,1)S(1)}, bf16[128,256]{1,0:T(8,128)(2,1)S(1)}, f32[192,128]{1,0:T(8,128)S(1)}) custom-call(bf16[128,256]{1,0:T(8,128)(2,1)S(1)} %bitcast.15, bf16[128,256]{1,0:T(8,128)(2,1)S(1)} %bitcast.16, bf16[128,256]{1,0:T(8,128)(2,1)S(1)} %bitcast.17, ...), custom_call_target="tpu_custom_call" | custom-call | tf_op jit(solution)/shard_map/pallas_call | solution.py:550
  90.3 0.0 copy-start.1
  90.3 0.6 copy-done.1
  90.9 0.0 copy-start.5
  90.9 0.6 copy-done.5
  91.5 0.0 copy-start.6
  91.5 0.6 copy-done.6
  92.2 0.0 copy-start.7
  92.2 0.6 copy-done.7
  92.8 0.0 copy-start.9
  92.8 0.6 copy-done.9
  93.4 1.8 %shard_map.93 = (bf16[192,128]{1,0:T(8,128)(2,1)}, bf16[128,256]{1,0:T(8,128)(2,1)}, bf16[128,256]{1,0:T(8,128)(2,1)}, bf16[128,256]{1,0:T(8,128)(2,1)}, f32[192,128]{1,0:T(8,128)}) custom-call(bf16[192,128]{1,0:T(8,128)(2,1)} %copy-done.9, bf16[128,256]{1,0:T(8,128)(2,1)} %copy-done.5, bf16[128,256]{1,0:T(8,128)(2,1)} %copy-done.6, ...), custom_call_target="tpu_custom_call" | custom-call | tf_op jit(solution)/shard_map/pallas_call | solution.py:600
Async XLA Ops:
  0.6 0.9 copy-start
  1.5 0.8 copy-start.2
  2.4 0.8 copy-start.3
  3.2 0.8 copy-start.4
  4.0 0.8 copy-start.8
  90.3 0.6 copy-start.1
  90.9 0.6 copy-start.5
  91.5 0.6 copy-start.6
  92.2 0.6 copy-start.7
  92.8 0.6 copy-start.9

commit v4 on v3

--- a/solution.py
+++ b/solution.py
@@ -171,9 +171,8 @@
         slots[0] += count
         return slots[0] - count
 
-    def send(src, dst, landed, peer, sends=None, receives=None, index=None, hears=None):
+    def send(src, dst, landed, peer, sends=None, receives=None, index=None):
         index = take(1) if index is None else index
-        hears = index if hears is None else hears
 
         def describe(source, target, which):
             return pltpu.make_async_remote_copy(
@@ -189,9 +188,11 @@
         issued.append(
             lambda: when(sends, lambda: describe(src, dst, index).wait_send())
         )
+        if landed is None:
+            return None
         return lambda inside=False: when(
             None if inside else receives,
-            lambda: describe(landed, landed, hears).wait_recv(),
+            lambda: describe(landed, landed, index).wait_recv(),
         )
 
     def wait(handles, *inside):
@@ -291,7 +292,7 @@
         send(
             hz.at[d],
             hr.at[e],
-            hr.at[e],
+            None,
             {"col": target * n + x},
             target != u,
             index=u_base + e,
@@ -594,7 +595,7 @@
             pltpu.SemaphoreType.DMA((copies,)),
         ],
         compiler_params=pltpu.CompilerParams(
-            collective_id=0, has_side_effects=True, vmem_limit_bytes=48 << 20
+            collective_id=0, has_side_effects=True, vmem_limit_bytes=64 << 20
         ),
     )(queries[0], key_vectors[0], value_vectors[0], out_weight.T, out_grad[0].T)
     result = pl.pallas_call(

time: 95.7 us -> 88.9 us (0.929)
  local copies, waits for them, and re-layouts: 7.3 us -> 0 us
    unnamed x20 -> x0, local copies, waits for them, and re-layouts: 7.3 us -> none
where the time goes in v4:
time: 88.9 us; the launch traced here: 88.6 us
  Pallas kernels  88 us (99%)
    pallas_call x1, Pallas kernels, shards(): pl.pallas_call(functools.partial(kernel, n, rows, cols), out_shape=(jax.S...  86.2 us
    pallas_call x1, Pallas kernels, shards(): pl.pallas_call(store_all, out_shape=[jax.ShapeDtypeStruct(a.shape, a.dtyp...  1.79 us

profile of v4, /device:TPU:1, one launch (start us, length us, event | category | flops | bytes accessed | tf_op | source)
XLA Modules:
  0.0 88.6 jit_solution(4402135156878134250)
XLA Ops:
  0.6 86.2 %shard_map.92 = (bf16[192,128]{1,0:T(8,128)(2,1)}, bf16[128,256]{1,0:T(8,128)(2,1)}, bf16[128,256]{1,0:T(8,128)(2,1)}, bf16[128,256]{1,0:T(8,128)(2,1)}, f32[192,128]{1,0:T(8,128)}) custom-call(bf16[128,256]{1,0:T(8,128)(2,1)} %bitcast.15, bf16[128,256]{1,0:T(8,128)(2,1)} %bitcast.16, bf16[128,256]{1,0:T(8,128)(2,1)} %bitcast.17, bf16[192,256]{1,0:T(8,128)(2,1)} %bitcast.14, ...), custom_call_target="tpu_custom_call" | custom-call | tf_op jit(solution)/shard_map/pallas_call | solution.py:551
  86.8 1.8 %shard_map.93 = (bf16[192,128]{1,0:T(8,128)(2,1)}, bf16[128,256]{1,0:T(8,128)(2,1)}, bf16[128,256]{1,0:T(8,128)(2,1)}, bf16[128,256]{1,0:T(8,128)(2,1)}, f32[192,128]{1,0:T(8,128)}) custom-call(bf16[192,128]{1,0:T(8,128)(2,1)} %get-tuple-element.15.refs_0_, bf16[128,256]{1,0:T(8,128)(2,1)} %get-tuple-element.16.refs_1_, ...), custom_call_target="tpu_custom_call" | custom-call | tf_op jit(solution)/shard_map/pallas_call | solution.py:601

commit v5 on v4

--- a/solution.py
+++ b/solution.py
@@ -65,6 +65,7 @@
     hx,
     hz,
     hr,
+    hq,
     of,
     top_ref,
     sum_ref,
@@ -150,7 +151,8 @@
 
     barrier = pltpu.get_barrier_semaphore()
     peers = [dp_peer] + [{"row": z_row(h, t)} for h, t in z_steps]
-    peers += [f(d) for f in (u_peer, y_peer, x_peer) for d in far]
+    peers += [u_peer(d) for d in sorted({1, n - 1})]
+    peers += [f(d) for f in (y_peer, x_peer) for d in far]
     for peer in peers:
         pl.semaphore_signal(
             barrier, inc=1, device_id=peer, device_id_type=pl.DeviceIdType.MESH
@@ -268,35 +270,33 @@
     g_s()
     gf[...] = flip(gt[...])
 
-    h_x = {}
+    x_base = take(n * (n - 1))
+
+    def x_send(d, e):
+        index = x_base + d * (n - 1) + e - 1
+        send(hs.at[d, e], hx.at[d, e - 1], None, x_peer(e), index=index)
 
     def head_terms(d):
         w_d[d]()
         for e in far + [0]:
             hs[d, e] = dot(gf[...], wf[at(y, d) * n + at(x, e)]).astype(BF16)
             if e:
-                h_x[d, e] = send(
-                    hs.at[d, e], hx.at[d, e - 1], hx.at[d, e - 1], x_peer(e)
-                )
-
-    u_base = take(n)
-
-    def head_sums(d):
+                x_send(d, e)
+
+    def head_sums(e):
+        d = lax.rem(u + e - y + n, n)
         total = hs[d, 0].astype(F32)
-        for e in far:
-            h_x[d, e]()
-            total = total + hx[d, e - 1].astype(F32)
-        hz[d] = total.astype(BF16)
-        target = at(y, d)
-        e = lax.rem(target - u + n, n)
-        send(
-            hz.at[d],
-            hr.at[e],
-            None,
-            {"col": target * n + x},
-            target != u,
-            index=u_base + e,
-        )
+        for k in far:
+            pltpu.make_async_remote_copy(
+                src_ref=hx.at[d, k - 1],
+                dst_ref=hx.at[d, k - 1],
+                send_sem=send_sems.at[x_base + d * (n - 1) + k - 1],
+                recv_sem=recv_sems.at[x_base + d * (n - 1) + k - 1],
+                device_id=x_peer(k),
+                device_id_type=pl.DeviceIdType.MESH,
+            ).wait_recv()
+            total = total + hx[d, k - 1].astype(F32)
+        return total
 
     head_terms(0)
 
@@ -331,8 +331,6 @@
     for d in near:
         head_terms(n - d)
     q_z = spread_z(qf.at[block(row), :], qs, lambda i: qf.at[block(i), :], z_steps[1:])
-    head_sums(0)
-
     for d in near:
 
         @pl.when(y >= d)
@@ -345,42 +343,66 @@
     total = sum_ref[:, :1]
     of[own_of] = (acc_ref[...] / total).astype(BF16)
     log_norm = top_ref[:, :1] + jnp.log(total)
-    o_u = {
-        d: send(of.at[own_of], of.at[own_of], of.at[x * n + at(u, -d)], u_peer(d))
-        for d in far
-    }
+    last = n - 1
+    low, high = slice(0, rows), slice(rows, span)
+    before, after = x * n + at(u, -1), x * n + at(u, 1)
+    beyond = x * n + at(u, 2)
+
+    o_u = [send(of.at[own_of], of.at[own_of], of.at[before], u_peer(1))]
+    if n > 2:
+        o_u.append(send(of.at[own_of], of.at[own_of], of.at[after], u_peer(last)))
 
     def spread_x(e):
         return [
             send(
-                of.at[x * n + at(u, -e)],
-                of.at[x * n + at(u, -e)],
-                of.at[at(x, -d) * n + at(u, -e)],
+                of.at[x * n + at(u, e)],
+                of.at[x * n + at(u, e)],
+                of.at[at(x, -d) * n + at(u, e)],
                 x_peer(d),
             )
             for d in far
         ]
 
     o_x = spread_x(0)
-    for d in near:
-        head_sums(n - d)
+    h_u = []
+    if n > 2:
+        hz[2] = head_sums(2).astype(BF16)
+        relay = [
+            send(hz.at[2, low, :], hq.at[0], hq.at[0], u_peer(1)),
+            send(hz.at[2, high, :], hq.at[1], hq.at[1], u_peer(last)),
+        ]
+        for e, part in ((1, high), (last, low)):
+            hz[e] = head_sums(e).astype(BF16)
+            h_u.append(
+                send(hz.at[e, part, :], hr.at[e, part, :], hr.at[e, part, :], u_peer(e))
+            )
+        for i, e, part in ((0, 1, low), (1, last, high)):
+            relay[i]()
+            hz[e, part, :] = (hz[e, part, :].astype(F32) + hq[i].astype(F32)).astype(
+                BF16
+            )
+            h_u.append(
+                send(hz.at[e, part, :], hr.at[e, part, :], hr.at[e, part, :], u_peer(e))
+            )
+    else:
+        hz[1] = head_sums(1).astype(BF16)
+        h_u.append(send(hz.at[1], hr.at[1], hr.at[1], u_peer(1)))
+    o_far = []
+    o_u[0]()
+    if n > 2:
+        o_far.append(
+            send(of.at[before, low, :], of.at[before, low, :], of.at[beyond, low, :], u_peer(1))
+        )
+        o_u[1]()
+        o_far.append(
+            send(of.at[after, high, :], of.at[after, high, :], of.at[beyond, high, :], u_peer(last))
+        )
+        o_x += spread_x(1)
+    o_x += spread_x(-1)
+    upstream = head_sums(0)
     q_y = gather_full(q_z, lambda i: qf.at[span_of(i), :], False)
-
-    for d in near:
-        o_u[d]()
-        o_x += spread_x(d)
-
-    for e in others:
-        pltpu.make_async_remote_copy(
-            src_ref=hr.at[e],
-            dst_ref=hr.at[e],
-            send_sem=send_sems.at[u_base + e],
-            recv_sem=recv_sems.at[u_base + e],
-            device_id=u_peer(e),
-            device_id_type=pl.DeviceIdType.MESH,
-        ).wait_recv()
-    upstream = hz[lax.rem(u - y + n, n)].astype(F32)
-    for e in others:
+    wait(h_u)
+    for e in sorted({1, last}):
         upstream = upstream + hr[e].astype(F32)
     df[span_of(pair), :] = upstream.astype(BF16)
     d_h = gather_h(lambda i: df.at[span_of(i), :])
@@ -401,6 +423,9 @@
         s_h[h - 1]()
         s_y.append(gather_y(lambda i: st.at[:, span_of(i)], h, False))
 
+    if n > 2:
+        wait(o_far)
+        o_x += spread_x(2)
     wait(o_x)
 
     def weight_part(which, target_y):
@@ -576,6 +601,7 @@
             buffer(n, n - 1, span, HEAD),
             buffer(n, span, HEAD),
             buffer(n, span, HEAD),
+            buffer(2, rows, HEAD),
             buffer(blocks, span, HEAD),
             buffer(span, HEAD, kind=F32),
             buffer(span, HEAD, kind=F32),

time: 88.9 us -> 81.7 us (0.919)
  Pallas kernels: 88 us -> 80.9 us
    pallas_call x1, Pallas kernels: 86.2 us -> 79.1 us  [shards(): pl.pallas_call(functools.partial(kernel, n, rows, cols), out_shape=(jax.S...]
where the time goes in v5:
time: 81.7 us; the launch traced here: 81.5 us
  Pallas kernels  80.9 us (99%)
    pallas_call x1, Pallas kernels, shards(): pl.pallas_call(functools.partial(kernel, n, rows, cols), out_shape=(jax.S...  79.1 us
    pallas_call x1, Pallas kernels, shards(): pl.pallas_call(store_all, out_shape=[jax.ShapeDtypeStruct(a.shape, a.dtyp...  1.79 us

profile of v5, /device:TPU:1, one launch (start us, length us, event | category | flops | bytes accessed | tf_op | source)
XLA Modules:
  0.0 81.5 jit_solution(18345217797685087940)
XLA Ops:
  0.6 79.1 %shard_map.92 = (bf16[192,128]{1,0:T(8,128)(2,1)}, bf16[128,256]{1,0:T(8,128)(2,1)}, bf16[128,256]{1,0:T(8,128)(2,1)}, bf16[128,256]{1,0:T(8,128)(2,1)}, f32[192,128]{1,0:T(8,128)}) custom-call(bf16[128,256]{1,0:T(8,128)(2,1)} %bitcast.15, bf16[128,256]{1,0:T(8,128)(2,1)} %bitcast.16, bf16[128,256]{1,0:T(8,128)(2,1)} %bitcast.17, bf16[192,256]{1,0:T(8,128)(2,1)} %bitcast.14, ...), custom_call_target="tpu_custom_call" | custom-call | tf_op jit(solution)/shard_map/pallas_call | solution.py:576
  79.7 1.8 %shard_map.93 = (bf16[192,128]{1,0:T(8,128)(2,1)}, bf16[128,256]{1,0:T(8,128)(2,1)}, bf16[128,256]{1,0:T(8,128)(2,1)}, bf16[128,256]{1,0:T(8,128)(2,1)}, f32[192,128]{1,0:T(8,128)}) custom-call(bf16[192,128]{1,0:T(8,128)(2,1)} %get-tuple-element.15.refs_0_, bf16[128,256]{1,0:T(8,128)(2,1)} %get-tuple-element.16.refs_1_, ...), custom_call_target="tpu_custom_call" | custom-call | tf_op jit(solution)/shard_map/pallas_call | solution.py:627

commit v6 on v5

--- a/solution.py
+++ b/solution.py
@@ -259,14 +259,17 @@
         wf.at[row, mine, :], ws.at[mine, :], lambda i: wf.at[i, mine, :], z_steps
     )
     g_s = send(gt.at[:, own_lanes], gt.at[:, own_lanes], gt.at[:, other_lanes], twin)
-    k_z = spread_z(kf.at[block(row), :], ks, lambda i: kf.at[block(i), :], z_steps)
+    w_parts = []
+    for h in range(m):
+        wait([w_z[step] for step in z_steps if step[0] == h])
+        w_parts.append(gather_y(w_pair, h, None))
+        if h == 0:
+            k_z = spread_z(
+                kf.at[block(row), :], ks, lambda i: kf.at[block(i), :], z_steps
+            )
+    w_d = {0: send(w_group(y), w_group(y), w_group(y, theirs), dp_peer)}
     q_s = spread_z(qf.at[block(row), :], qs, lambda i: qf.at[block(i), :], z_steps[:1])
     v_z = spread_z(vf.at[block(row), :], vs, lambda i: vf.at[block(i), :], z_steps)
-
-    w_y = gather_full(w_z, w_pair, None)
-    w_d = {0: send(w_group(y), w_group(y), w_group(y, theirs), dp_peer)}
-    k_y = gather_full(k_z, lambda i: kf.at[span_of(i), :], True)
-    v_y = gather_full(v_z, lambda i: vf.at[span_of(i), :], True)
     g_s()
     gf[...] = flip(gt[...])
 
@@ -299,6 +302,8 @@
         return total
 
     head_terms(0)
+    k_y = gather_full(k_z, lambda i: kf.at[span_of(i), :], True)
+    v_y = gather_full(v_z, lambda i: vf.at[span_of(i), :], True)
 
     query_pos = pair * span + lax.broadcasted_iota(jnp.int32, (span, chunk), 0)
     key_pos = y * chunk + lax.broadcasted_iota(jnp.int32, (span, chunk), 1)
@@ -323,7 +328,7 @@
         acc_ref[...] = acc
 
     for d in near:
-        wait(w_y[d])
+        wait([part[d] for part in w_parts])
         source = at(y, -d)
         w_d[n - d] = send(w_group(source), w_group(source), w_group(source, theirs), dp_peer)
     wait(q_s.values())
@@ -363,7 +368,7 @@
             for d in far
         ]
 
-    o_x = spread_x(0)
+    o_x = {0: spread_x(0)}
     h_u = []
     if n > 2:
         hz[2] = head_sums(2).astype(BF16)
@@ -397,10 +402,45 @@
         o_far.append(
             send(of.at[after, high, :], of.at[after, high, :], of.at[beyond, high, :], u_peer(last))
         )
-        o_x += spread_x(1)
-    o_x += spread_x(-1)
+        o_x[1] = spread_x(1)
+    o_x[last] = spread_x(-1)
+
+    y_base = take(n)
+
+    def weight_terms(e):
+        wait(o_x[e])
+        target = at(u, e)
+        for i in range(n):
+            gp[e, i] = dot(gt[...], of[i * n + target]).astype(BF16)
+        ours = target // m == dp
+        arrived = send(
+            gp.at[e], gd.at[e], gd.at[e], dp_peer, target // m != dp, ours
+        )
+        arrived()
+
+        @pl.when(ours)
+        def _():
+            for i in range(n):
+                gy[e, i] = (gp[e, i].astype(F32) + gd[e, i].astype(F32)).astype(BF16)
+
+        for i in range(2):
+            target_y = 2 * lax.rem(target, m) + i
+            d = lax.rem(target_y - y + n, n)
+            send(
+                gy.at[e, pl.ds(i * m, m)],
+                gyr.at[d],
+                None,
+                {"row": target_y * n + z},
+                jnp.logical_and(ours, target_y != y),
+                index=y_base + d,
+            )
+
+    weight_terms(0)
     upstream = head_sums(0)
     q_y = gather_full(q_z, lambda i: qf.at[span_of(i), :], False)
+    if n > 2:
+        wait(o_far)
+        o_x[2] = spread_x(2)
     wait(h_u)
     for e in sorted({1, last}):
         upstream = upstream + hr[e].astype(F32)
@@ -417,57 +457,6 @@
     s_h = gather_h(lambda i: st.at[:, span_of(i)])
     s_y = [gather_y(lambda i: st.at[:, span_of(i)], 0, False)]
 
-    for h in range(1, m):
-        d_h[h - 1]()
-        d_y.append(gather_y(lambda i: df.at[span_of(i), :], h, False))
-        s_h[h - 1]()
-        s_y.append(gather_y(lambda i: st.at[:, span_of(i)], h, False))
-
-    if n > 2:
-        wait(o_far)
-        o_x += spread_x(2)
-    wait(o_x)
-
-    def weight_part(which, target_y):
-        first = which * n * m + target_y * m
-        for i in range(m):
-            c = first + i
-            part = dot(gt[...], of[lax.rem(c, n) * n + c // n])
-            gp[c] = part.astype(BF16)
-
-    g_d = {}
-    for d in far + [0]:
-        target_y = at(y, d)
-        weight_part(1 - dp, target_y)
-        away = pl.ds((1 - dp) * n * m + target_y * m, m)
-        here = pl.ds(target_y * m, m)
-        g_d[d] = send(gp.at[away], gd.at[here], gd.at[here], dp_peer)
-    for d in far + [0]:
-        weight_part(dp, at(y, d))
-
-    g_y = []
-    for d in far + [0]:
-        target_y = at(y, d)
-        g_d[d]()
-        for i in range(m):
-            slot = target_y * m + i
-            gy[slot] = (
-                gp[dp * n * m + slot].astype(F32) + gd[slot].astype(F32)
-            ).astype(BF16)
-        if d:
-            here = pl.ds(target_y * m, m)
-            g_y.append(send(gy.at[here], gyr.at[d - 1], gyr.at[d - 1], y_peer(d)))
-
-    lanes = [slice(h * HEAD, (h + 1) * HEAD) for h in range(2)]
-
-    def project(c, acc):
-        return acc + dot_nt(wf[c], of[lax.rem(c, n) * n + c // n])
-
-    projected = lax.fori_loop(0, n * n, project, jnp.zeros((cols, span), F32))
-    for h in range(2):
-        ox[h] = projected[:, lanes[h]].astype(BF16)
-    o_s = send(ox.at[1 - side], oxr, oxr, twin)
-
     def queries_pass(j, first, acc):
         keys = kf[group(j), :]
         scores = dot_nt(qf[span_of(pair), :], keys) * SCALE
@@ -478,22 +467,31 @@
         slopes = (probs * (slopes - row_dot)).astype(BF16)
         return acc + dot(slopes, keys)
 
+    weight_terms(last)
+    for h in range(1, m):
+        d_h[h - 1]()
+        d_y.append(gather_y(lambda i: df.at[span_of(i), :], h, False))
+        s_h[h - 1]()
+        s_y.append(gather_y(lambda i: st.at[:, span_of(i)], h, False))
+    if n > 2:
+        weight_terms(1)
     acc = queries_pass(y, True, jnp.zeros((span, HEAD), F32))
     acc = lax.fori_loop(0, y, lambda j, acc: queries_pass(j, False, acc), acc)
     acc = (acc * SCALE).astype(BF16)
     dx[0, 0], dx[0, 1] = acc[:rows], acc[rows:]
     swaps = [send(dx.at[0, 1 - side], dxr.at[0], dxr.at[0], twin)]
-
-    wait(g_y)
-    g_z = []
-    for d in list(range(1, m)) + [0]:
-        target = at_h(d)
-        total = gy[y * m + target].astype(F32)
-        for e in others:
-            total = total + gyr[e - 1, target].astype(F32)
-        gz[d] = total.astype(BF16)
-        if d:
-            g_z.append(send(gz.at[d], gzr.at[d - 1], gzr.at[d - 1], h_peer(d)))
+    if n > 2:
+        weight_terms(2)
+
+    lanes = [slice(h * HEAD, (h + 1) * HEAD) for h in range(2)]
+
+    def project(c, acc):
+        return acc + dot_nt(wf[c], of[lax.rem(c, n) * n + c // n])
+
+    projected = lax.fori_loop(0, n * n, project, jnp.zeros((cols, span), F32))
+    for h in range(2):
+        ox[h] = projected[:, lanes[h]].astype(BF16)
+    o_s = send(ox.at[1 - side], oxr, oxr, twin)
 
     own_key = pair * span + lax.broadcasted_iota(jnp.int32, (span, chunk), 0)
     ask_pos = y * chunk + lax.broadcasted_iota(jnp.int32, (span, chunk), 1)
@@ -517,6 +515,27 @@
             sum_ref[...] += sum_v
 
     keys_pass(y, True)
+
+    for d in others:
+        pltpu.make_async_remote_copy(
+            src_ref=gyr.at[d],
+            dst_ref=gyr.at[d],
+            send_sem=send_sems.at[y_base + d],
+            recv_sem=recv_sems.at[y_base + d],
+            device_id=y_peer(d),
+            device_id_type=pl.DeviceIdType.MESH,
+        ).wait_recv()
+    own_e = lax.rem(dp * m + y // 2 - u + n, n)
+    own_i = lax.rem(y, 2) * m
+    g_z = []
+    for d in list(range(1, m)) + [0]:
+        target = at_h(d)
+        total = gy[own_e, own_i + target].astype(F32)
+        for e in others:
+            total = total + gyr[e, target].astype(F32)
+        gz[d] = total.astype(BF16)
+        if d:
+            g_z.append(send(gz.at[d], gzr.at[d - 1], gzr.at[d - 1], h_peer(d)))
     for d in near:
 
         @pl.when(y + d < n)
@@ -606,10 +625,10 @@
             buffer(span, HEAD, kind=F32),
             buffer(span, HEAD, kind=F32),
             buffer(span, HEAD, kind=F32),
-            buffer(blocks, cols, HEAD),
-            buffer(n * m, cols, HEAD),
-            buffer(n * m, cols, HEAD),
-            buffer(n - 1, m, cols, HEAD),
+            buffer(n, n, cols, HEAD),
+            buffer(n, n, cols, HEAD),
+            buffer(n, n, cols, HEAD),
+            buffer(n, m, cols, HEAD),
             buffer(m, cols, HEAD),
             buffer(max(m - 1, 1), cols, HEAD),
             buffer(2, cols, rows),

time: 81.7 us -> 81 us (level)
  no operation moved by 1% of the time
where the time goes in v6:
time: 81 us; the launch traced here: 80.8 us
  Pallas kernels  80.1 us (99%)
    pallas_call x1, Pallas kernels, shards(): pl.pallas_call(functools.partial(kernel, n, rows, cols), out_shape=(jax.S...  78.3 us
    pallas_call x1, Pallas kernels, shards(): pl.pallas_call(store_all, out_shape=[jax.ShapeDtypeStruct(a.shape, a.dtyp...  1.79 us

profile of v6, /device:TPU:1, one launch (start us, length us, event | category | flops | bytes accessed | tf_op | source)
XLA Modules:
  0.0 80.8 jit_solution(6068421773112782573)
XLA Ops:
  0.6 78.3 %shard_map.92 = (bf16[192,128]{1,0:T(8,128)(2,1)}, bf16[128,256]{1,0:T(8,128)(2,1)}, bf16[128,256]{1,0:T(8,128)(2,1)}, bf16[128,256]{1,0:T(8,128)(2,1)}, f32[192,128]{1,0:T(8,128)}) custom-call(bf16[128,256]{1,0:T(8,128)(2,1)} %bitcast.15, bf16[128,256]{1,0:T(8,128)(2,1)} %bitcast.16, bf16[128,256]{1,0:T(8,128)(2,1)} %bitcast.17, bf16[192,256]{1,0:T(8,128)(2,1)} %bitcast.14, ...), custom_call_target="tpu_custom_call" | custom-call | tf_op jit(solution)/shard_map/pallas_call | solution.py:595
  79.0 1.8 %shard_map.93 = (bf16[192,128]{1,0:T(8,128)(2,1)}, bf16[128,256]{1,0:T(8,128)(2,1)}, bf16[128,256]{1,0:T(8,128)(2,1)}, bf16[128,256]{1,0:T(8,128)(2,1)}, f32[192,128]{1,0:T(8,128)}) custom-call(bf16[192,128]{1,0:T(8,128)(2,1)} %get-tuple-element.15.refs_0_, bf16[128,256]{1,0:T(8,128)(2,1)} %get-tuple-element.16.refs_1_, ...), custom_call_target="tpu_custom_call" | custom-call | tf_op jit(solution)/shard_map/pallas_call | solution.py:646

commit v7 on v6

--- a/solution.py
+++ b/solution.py
@@ -61,8 +61,9 @@
     wf,
     gf,
     gt,
-    hs,
-    hx,
+    wx,
+    px,
+    pr,
     hz,
     hr,
     hq,
@@ -76,6 +77,7 @@
     gyr,
     gz,
     gzr,
+    gm,
     ox,
     oxr,
     dx,
@@ -139,7 +141,7 @@
     pieces = [
         (w_hbm.at[mine, own_lanes], wf.at[row, mine, :]),
         (w_hbm.at[mine, other_lanes], ws.at[mine, :]),
-        (g_hbm, gt.at[:, own_lanes]),
+        (g_hbm, gt.at[x, :, own_lanes]),
     ]
     for source, split, full in ((k_hbm, ks, kf), (q_hbm, qs, qf), (v_hbm, vs, vf)):
         pieces.append((source.at[:, own_lanes], full.at[block(row), :]))
@@ -153,6 +155,19 @@
     peers = [dp_peer] + [{"row": z_row(h, t)} for h, t in z_steps]
     peers += [u_peer(d) for d in sorted({1, n - 1})]
     peers += [f(d) for f in (y_peer, x_peer) for d in far]
+    code = lax.rem(y, 2) * m + zh
+    mirror = {
+        "row": (y - lax.rem(y, 2) + x // m) * n + 2 * lax.rem(x, m) + side,
+        "col": u * n + code,
+    }
+    moves = code != x
+
+    @pl.when(moves)
+    def _():
+        pl.semaphore_signal(
+            barrier, inc=1, device_id=mirror, device_id_type=pl.DeviceIdType.MESH
+        )
+
     for peer in peers:
         pl.semaphore_signal(
             barrier, inc=1, device_id=peer, device_id_type=pl.DeviceIdType.MESH
@@ -249,16 +264,15 @@
     def w_pair(i):
         return wf.at[pl.ds(2 * i, 2), mine, :]
 
-    def w_group(i, part=mine):
-        return wf.at[pl.ds(i * n, n), part, :]
-
     wait([load.wait for load in loads])
-    pl.semaphore_wait(barrier, len(peers))
+    pl.semaphore_wait(barrier, len(peers) + jnp.where(moves, 1, 0))
 
     w_z = spread_z(
         wf.at[row, mine, :], ws.at[mine, :], lambda i: wf.at[i, mine, :], z_steps
     )
-    g_s = send(gt.at[:, own_lanes], gt.at[:, own_lanes], gt.at[:, other_lanes], twin)
+    g_s = send(
+        gt.at[x, :, own_lanes], gt.at[x, :, own_lanes], gt.at[x, :, other_lanes], twin
+    )
     w_parts = []
     for h in range(m):
         wait([w_z[step] for step in z_steps if step[0] == h])
@@ -267,43 +281,53 @@
             k_z = spread_z(
                 kf.at[block(row), :], ks, lambda i: kf.at[block(i), :], z_steps
             )
-    w_d = {0: send(w_group(y), w_group(y), w_group(y, theirs), dp_peer)}
+
+    def w_across(i):
+        j = at(y, i)
+        wx[j, x, mine, :] = wf[j * n + x, mine, :]
+        return [
+            send(
+                wf.at[j * n + at(x, e), mine, :],
+                wx.at[j, x, mine, :],
+                wx.at[j, at(x, -e), mine, :],
+                x_peer(e),
+            )
+            for e in far
+        ]
+
+    w_x = {0: w_across(0)}
     q_s = spread_z(qf.at[block(row), :], qs, lambda i: qf.at[block(i), :], z_steps[:1])
     v_z = spread_z(vf.at[block(row), :], vs, lambda i: vf.at[block(i), :], z_steps)
     g_s()
-    gf[...] = flip(gt[...])
-
-    x_base = take(n * (n - 1))
-
-    def x_send(d, e):
-        index = x_base + d * (n - 1) + e - 1
-        send(hs.at[d, e], hx.at[d, e - 1], None, x_peer(e), index=index)
-
-    def head_terms(d):
-        w_d[d]()
-        for e in far + [0]:
-            hs[d, e] = dot(gf[...], wf[at(y, d) * n + at(x, e)]).astype(BF16)
-            if e:
-                x_send(d, e)
-
-    def head_sums(e):
-        d = lax.rem(u + e - y + n, n)
-        total = hs[d, 0].astype(F32)
-        for k in far:
-            pltpu.make_async_remote_copy(
-                src_ref=hx.at[d, k - 1],
-                dst_ref=hx.at[d, k - 1],
-                send_sem=send_sems.at[x_base + d * (n - 1) + k - 1],
-                recv_sem=recv_sems.at[x_base + d * (n - 1) + k - 1],
-                device_id=x_peer(k),
-                device_id_type=pl.DeviceIdType.MESH,
-            ).wait_recv()
-            total = total + hx[d, k - 1].astype(F32)
-        return total
-
-    head_terms(0)
+    g_x = {
+        e: send(gt.at[x], gt.at[x], gt.at[at(x, -e)], x_peer(e)) for e in far
+    }
+    gf[x] = flip(gt[x])
     k_y = gather_full(k_z, lambda i: kf.at[span_of(i), :], True)
     v_y = gather_full(v_z, lambda i: vf.at[span_of(i), :], True)
+
+    d_base = take(n)
+
+    def w_swap(i):
+        wait(w_x[i])
+        j = at(y, i)
+        send(wx.at[j, :, mine, :], wx.at[j, :, mine, :], None, dp_peer, index=d_base + i)
+
+    def head_sums(e):
+        j = at(u, e)
+        i = lax.rem(j - y + n, n)
+        pltpu.make_async_remote_copy(
+            src_ref=wx.at[j, :, theirs, :],
+            dst_ref=wx.at[j, :, theirs, :],
+            send_sem=send_sems.at[d_base + i],
+            recv_sem=recv_sems.at[d_base + i],
+            device_id=dp_peer,
+            device_id_type=pl.DeviceIdType.MESH,
+        ).wait_recv()
+        total = dot(gf[0], wx[j, 0])
+        for k in others:
+            total = total + dot(gf[k], wx[j, k])
+        return total
 
     query_pos = pair * span + lax.broadcasted_iota(jnp.int32, (span, chunk), 0)
     key_pos = y * chunk + lax.broadcasted_iota(jnp.int32, (span, chunk), 1)
@@ -329,46 +353,19 @@
 
     for d in near:
         wait([part[d] for part in w_parts])
-        source = at(y, -d)
-        w_d[n - d] = send(w_group(source), w_group(source), w_group(source, theirs), dp_peer)
+        w_x[n - d] = w_across(n - d)
     wait(q_s.values())
     forward(y, True)
+    w_swap(0)
+    for e in near:
+        g_x[e]()
+        gf[at(x, -e)] = flip(gt[at(x, -e)])
     for d in near:
-        head_terms(n - d)
+        w_swap(n - d)
     q_z = spread_z(qf.at[block(row), :], qs, lambda i: qf.at[block(i), :], z_steps[1:])
-    for d in near:
-
-        @pl.when(y >= d)
-        def _(d=d):
-            wait(k_y[d], True)
-            wait(v_y[d], True)
-            forward(y - d, False)
-
-    own_of = x * n + u
-    total = sum_ref[:, :1]
-    of[own_of] = (acc_ref[...] / total).astype(BF16)
-    log_norm = top_ref[:, :1] + jnp.log(total)
+
     last = n - 1
     low, high = slice(0, rows), slice(rows, span)
-    before, after = x * n + at(u, -1), x * n + at(u, 1)
-    beyond = x * n + at(u, 2)
-
-    o_u = [send(of.at[own_of], of.at[own_of], of.at[before], u_peer(1))]
-    if n > 2:
-        o_u.append(send(of.at[own_of], of.at[own_of], of.at[after], u_peer(last)))
-
-    def spread_x(e):
-        return [
-            send(
-                of.at[x * n + at(u, e)],
-                of.at[x * n + at(u, e)],
-                of.at[at(x, -d) * n + at(u, e)],
-                x_peer(d),
-            )
-            for d in far
-        ]
-
-    o_x = {0: spread_x(0)}
     h_u = []
     if n > 2:
         hz[2] = head_sums(2).astype(BF16)
@@ -381,6 +378,30 @@
             h_u.append(
                 send(hz.at[e, part, :], hr.at[e, part, :], hr.at[e, part, :], u_peer(e))
             )
+    else:
+        hz[1] = head_sums(1).astype(BF16)
+        h_u.append(send(hz.at[1], hr.at[1], hr.at[1], u_peer(1)))
+    upstream = head_sums(0)
+
+    for d in near:
+
+        @pl.when(y >= d)
+        def _(d=d):
+            wait(k_y[d], True)
+            wait(v_y[d], True)
+            forward(y - d, False)
+
+    own_of = u
+    total = sum_ref[:, :1]
+    of[own_of] = (acc_ref[...] / total).astype(BF16)
+    log_norm = top_ref[:, :1] + jnp.log(total)
+    before, after, beyond = at(u, -1), at(u, 1), at(u, 2)
+
+    o_u = [send(of.at[own_of], of.at[own_of], of.at[before], u_peer(1))]
+    if n > 2:
+        o_u.append(send(of.at[own_of], of.at[own_of], of.at[after], u_peer(last)))
+
+    if n > 2:
         for i, e, part in ((0, 1, low), (1, last, high)):
             relay[i]()
             hz[e, part, :] = (hz[e, part, :].astype(F32) + hq[i].astype(F32)).astype(
@@ -389,9 +410,6 @@
             h_u.append(
                 send(hz.at[e, part, :], hr.at[e, part, :], hr.at[e, part, :], u_peer(e))
             )
-    else:
-        hz[1] = head_sums(1).astype(BF16)
-        h_u.append(send(hz.at[1], hr.at[1], hr.at[1], u_peer(1)))
     o_far = []
     o_u[0]()
     if n > 2:
@@ -402,16 +420,13 @@
         o_far.append(
             send(of.at[after, high, :], of.at[after, high, :], of.at[beyond, high, :], u_peer(last))
         )
-        o_x[1] = spread_x(1)
-    o_x[last] = spread_x(-1)
 
     y_base = take(n)
 
     def weight_terms(e):
-        wait(o_x[e])
         target = at(u, e)
         for i in range(n):
-            gp[e, i] = dot(gt[...], of[i * n + target]).astype(BF16)
+            gp[e, i] = dot(gt[i], of[target]).astype(BF16)
         ours = target // m == dp
         arrived = send(
             gp.at[e], gd.at[e], gd.at[e], dp_peer, target // m != dp, ours
@@ -436,11 +451,7 @@
             )
 
     weight_terms(0)
-    upstream = head_sums(0)
     q_y = gather_full(q_z, lambda i: qf.at[span_of(i), :], False)
-    if n > 2:
-        wait(o_far)
-        o_x[2] = spread_x(2)
     wait(h_u)
     for e in sorted({1, last}):
         upstream = upstream + hr[e].astype(F32)
@@ -467,31 +478,37 @@
         slopes = (probs * (slopes - row_dot)).astype(BF16)
         return acc + dot(slopes, keys)
 
-    weight_terms(last)
+    if n > 2:
+        weight_terms(1)
     for h in range(1, m):
         d_h[h - 1]()
         d_y.append(gather_y(lambda i: df.at[span_of(i), :], h, False))
         s_h[h - 1]()
         s_y.append(gather_y(lambda i: st.at[:, span_of(i)], h, False))
-    if n > 2:
-        weight_terms(1)
+    weight_terms(last)
     acc = queries_pass(y, True, jnp.zeros((span, HEAD), F32))
     acc = lax.fori_loop(0, y, lambda j, acc: queries_pass(j, False, acc), acc)
     acc = (acc * SCALE).astype(BF16)
     dx[0, 0], dx[0, 1] = acc[:rows], acc[rows:]
     swaps = [send(dx.at[0, 1 - side], dxr.at[0], dxr.at[0], twin)]
     if n > 2:
+        wait(o_far)
         weight_terms(2)
 
     lanes = [slice(h * HEAD, (h + 1) * HEAD) for h in range(2)]
 
-    def project(c, acc):
-        return acc + dot_nt(wf[c], of[lax.rem(c, n) * n + c // n])
-
-    projected = lax.fori_loop(0, n * n, project, jnp.zeros((cols, span), F32))
-    for h in range(2):
-        ox[h] = projected[:, lanes[h]].astype(BF16)
-    o_s = send(ox.at[1 - side], oxr, oxr, twin)
+    def project(i):
+        total = dot_nt(wx[0, i], of[0])
+        for j in others:
+            total = total + dot_nt(wx[j, i], of[j])
+        return total
+
+    p_x = []
+    for e in far:
+        target_x = at(x, e)
+        px[e] = project(target_x).astype(BF16)
+        p_x.append(send(px.at[e], pr.at[e], pr.at[e], x_peer(e)))
+    projected = project(x)
 
     own_key = pair * span + lax.broadcasted_iota(jnp.int32, (span, chunk), 0)
     ask_pos = y * chunk + lax.broadcasted_iota(jnp.int32, (span, chunk), 1)
@@ -515,6 +532,12 @@
             sum_ref[...] += sum_v
 
     keys_pass(y, True)
+    wait(p_x)
+    for e in others:
+        projected = projected + pr[e].astype(F32)
+    for h in range(2):
+        ox[h] = projected[:, lanes[h]].astype(BF16)
+    o_s = send(ox.at[1 - side], oxr, oxr, twin)
 
     for d in others:
         pltpu.make_async_remote_copy(
@@ -555,7 +578,8 @@
     total = gz[0].astype(F32)
     for d in range(1, m):
         total = total + gzr[d - 1].astype(F32)
-    gw_ref[...] = total
+    gm[0] = total.astype(BF16)
+    g_m = send(gm.at[0], gm.at[1], gm.at[1], mirror, moves, moves)
     o_s()
     out_ref[...] = (ox[side].astype(F32) + oxr[...].astype(F32)).astype(BF16)
     for i, target in enumerate((dq_ref, dk_ref, dv_ref)):
@@ -563,6 +587,13 @@
         own, other = dx[i, side], dxr[i]
         for h in range(2):
             target[:, lanes[h]] = jnp.where(side == h, own, other)
+
+    gw_ref[...] = total
+
+    @pl.when(moves)
+    def _():
+        g_m(True)
+        gw_ref[...] = gm[1].astype(F32)
 
     for finish in issued:
         finish()
@@ -614,14 +645,15 @@
             full,
             buffer(8, blocks * rows, kind=F32),
             buffer(blocks, cols, HEAD),
-            buffer(span, cols),
-            buffer(cols, span),
-            buffer(n, n, span, HEAD),
-            buffer(n, n - 1, span, HEAD),
+            buffer(n, span, cols),
+            buffer(n, cols, span),
+            buffer(n, n, cols, HEAD),
+            buffer(n, cols, span),
+            buffer(n, cols, span),
             buffer(n, span, HEAD),
             buffer(n, span, HEAD),
             buffer(2, rows, HEAD),
-            buffer(blocks, span, HEAD),
+            buffer(n, span, HEAD),
             buffer(span, HEAD, kind=F32),
             buffer(span, HEAD, kind=F32),
             buffer(span, HEAD, kind=F32),
@@ -631,6 +663,7 @@
             buffer(n, m, cols, HEAD),
             buffer(m, cols, HEAD),
             buffer(max(m - 1, 1), cols, HEAD),
+            buffer(2, cols, HEAD),
             buffer(2, cols, rows),
             buffer(cols, rows),
             buffer(3, 2, rows, HEAD),

time: 81 us -> 84.1 us (1.038)
  the two profiles are of different devices: /device:TPU:1 before, /device:TPU:22 now
where the time goes in v7:
time: 84.1 us; the launch traced here: 83.9 us
  Pallas kernels  83.3 us (99%)
    pallas_call x1, Pallas kernels, shards(): pl.pallas_call(functools.partial(kernel, n, rows, cols), out_shape=(jax.S...  81.5 us
    pallas_call x1, Pallas kernels, shards(): pl.pallas_call(store_all, out_shape=[jax.ShapeDtypeStruct(a.shape, a.dtyp...  1.79 us

profile of v7, /device:TPU:22, one launch (start us, length us, event | category | flops | bytes accessed | tf_op | source)
XLA Modules:
  0.0 83.9 jit_solution(17189225003452800947)
XLA Ops:
  0.6 81.5 %shard_map.92 = (bf16[192,128]{1,0:T(8,128)(2,1)}, bf16[128,256]{1,0:T(8,128)(2,1)}, bf16[128,256]{1,0:T(8,128)(2,1)}, bf16[128,256]{1,0:T(8,128)(2,1)}, f32[192,128]{1,0:T(8,128)}) custom-call(bf16[128,256]{1,0:T(8,128)(2,1)} %bitcast.15, bf16[128,256]{1,0:T(8,128)(2,1)} %bitcast.16, bf16[128,256]{1,0:T(8,128)(2,1)} %bitcast.17, bf16[192,256]{1,0:T(8,128)(2,1)} %bitcast.14, ...), custom_call_target="tpu_custom_call" | custom-call | tf_op jit(solution)/shard_map/pallas_call | solution.py:626
  82.1 1.8 %shard_map.93 = (bf16[192,128]{1,0:T(8,128)(2,1)}, bf16[128,256]{1,0:T(8,128)(2,1)}, bf16[128,256]{1,0:T(8,128)(2,1)}, bf16[128,256]{1,0:T(8,128)(2,1)}, f32[192,128]{1,0:T(8,128)}) custom-call(bf16[192,128]{1,0:T(8,128)(2,1)} %get-tuple-element.15.refs_0_, bf16[128,256]{1,0:T(8,128)(2,1)} %get-tuple-element.16.refs_1_, ...), custom_call_target="tpu_custom_call" | custom-call | tf_op jit(solution)/shard_map/pallas_call | solution.py:679

commit v8 on v7

--- a/solution.py
+++ b/solution.py
@@ -362,7 +362,6 @@
         gf[at(x, -e)] = flip(gt[at(x, -e)])
     for d in near:
         w_swap(n - d)
-    q_z = spread_z(qf.at[block(row), :], qs, lambda i: qf.at[block(i), :], z_steps[1:])
 
     last = n - 1
     low, high = slice(0, rows), slice(rows, span)
@@ -422,16 +421,21 @@
         )
 
     y_base = take(n)
+    g_d = {}
 
     def weight_terms(e):
         target = at(u, e)
         for i in range(n):
             gp[e, i] = dot(gt[i], of[target]).astype(BF16)
         ours = target // m == dp
-        arrived = send(
+        g_d[e] = send(
             gp.at[e], gd.at[e], gd.at[e], dp_peer, target // m != dp, ours
         )
-        arrived()
+
+    def weight_sums(e):
+        target = at(u, e)
+        ours = target // m == dp
+        g_d[e]()
 
         @pl.when(ours)
         def _():
@@ -450,8 +454,11 @@
                 index=y_base + d,
             )
 
+    q_z = spread_z(qf.at[block(row), :], qs, lambda i: qf.at[block(i), :], z_steps[1:])
     weight_terms(0)
-    q_y = gather_full(q_z, lambda i: qf.at[span_of(i), :], False)
+    weight_terms(last)
+    if n > 2:
+        weight_terms(1)
     wait(h_u)
     for e in sorted({1, last}):
         upstream = upstream + hr[e].astype(F32)
@@ -479,22 +486,16 @@
         return acc + dot(slopes, keys)
 
     if n > 2:
-        weight_terms(1)
+        wait(o_far)
+        weight_terms(2)
     for h in range(1, m):
         d_h[h - 1]()
         d_y.append(gather_y(lambda i: df.at[span_of(i), :], h, False))
         s_h[h - 1]()
         s_y.append(gather_y(lambda i: st.at[:, span_of(i)], h, False))
-    weight_terms(last)
-    acc = queries_pass(y, True, jnp.zeros((span, HEAD), F32))
-    acc = lax.fori_loop(0, y, lambda j, acc: queries_pass(j, False, acc), acc)
-    acc = (acc * SCALE).astype(BF16)
-    dx[0, 0], dx[0, 1] = acc[:rows], acc[rows:]
-    swaps = [send(dx.at[0, 1 - side], dxr.at[0], dxr.at[0], twin)]
-    if n > 2:
-        wait(o_far)
-        weight_terms(2)
-
+    for e in [0, last] + ([1, 2] if n > 2 else []):
+        weight_sums(e)
+    q_y = gather_full(q_z, lambda i: qf.at[span_of(i), :], False)
     lanes = [slice(h * HEAD, (h + 1) * HEAD) for h in range(2)]
 
     def project(i):
@@ -509,6 +510,12 @@
         px[e] = project(target_x).astype(BF16)
         p_x.append(send(px.at[e], pr.at[e], pr.at[e], x_peer(e)))
     projected = project(x)
+
+    acc = queries_pass(y, True, jnp.zeros((span, HEAD), F32))
+    acc = lax.fori_loop(0, y, lambda j, acc: queries_pass(j, False, acc), acc)
+    acc = (acc * SCALE).astype(BF16)
+    dx[0, 0], dx[0, 1] = acc[:rows], acc[rows:]
+    swaps = [send(dx.at[0, 1 - side], dxr.at[0], dxr.at[0], twin)]
 
     own_key = pair * span + lax.broadcasted_iota(jnp.int32, (span, chunk), 0)
     ask_pos = y * chunk + lax.broadcasted_iota(jnp.int32, (span, chunk), 1)
@@ -532,13 +539,6 @@
             sum_ref[...] += sum_v
 
     keys_pass(y, True)
-    wait(p_x)
-    for e in others:
-        projected = projected + pr[e].astype(F32)
-    for h in range(2):
-        ox[h] = projected[:, lanes[h]].astype(BF16)
-    o_s = send(ox.at[1 - side], oxr, oxr, twin)
-
     for d in others:
         pltpu.make_async_remote_copy(
             src_ref=gyr.at[d],
@@ -580,6 +580,13 @@
         total = total + gzr[d - 1].astype(F32)
     gm[0] = total.astype(BF16)
     g_m = send(gm.at[0], gm.at[1], gm.at[1], mirror, moves, moves)
+    wait(p_x)
+    for e in others:
+        projected = projected + pr[e].astype(F32)
+    for h in range(2):
+        ox[h] = projected[:, lanes[h]].astype(BF16)
+    o_s = send(ox.at[1 - side], oxr, oxr, twin)
+
     o_s()
     out_ref[...] = (ox[side].astype(F32) + oxr[...].astype(F32)).astype(BF16)
     for i, target in enumerate((dq_ref, dk_ref, dv_ref)):

time: 84.1 us -> 86.3 us (1.026)
  the two profiles are of different devices: /device:TPU:22 before, /device:TPU:1 now
where the time goes in v8:
time: 86.3 us; the launch traced here: 84.8 us
  Pallas kernels  84.1 us (97%)
    pallas_call x1, Pallas kernels, shards(): pl.pallas_call(functools.partial(kernel, n, rows, cols), out_shape=(jax.S...  82.3 us
    pallas_call x1, Pallas kernels, shards(): pl.pallas_call(store_all, out_shape=[jax.ShapeDtypeStruct(a.shape, a.dtyp...  1.79 us

profile of v8, /device:TPU:1, one launch (start us, length us, event | category | flops | bytes accessed | tf_op | source)
XLA Modules:
  0.0 84.8 jit_solution(11786831760623001834)
XLA Ops:
  0.6 82.3 %shard_map.92 = (bf16[192,128]{1,0:T(8,128)(2,1)}, bf16[128,256]{1,0:T(8,128)(2,1)}, bf16[128,256]{1,0:T(8,128)(2,1)}, bf16[128,256]{1,0:T(8,128)(2,1)}, f32[192,128]{1,0:T(8,128)}) custom-call(bf16[128,256]{1,0:T(8,128)(2,1)} %bitcast.15, bf16[128,256]{1,0:T(8,128)(2,1)} %bitcast.16, bf16[128,256]{1,0:T(8,128)(2,1)} %bitcast.17, bf16[192,256]{1,0:T(8,128)(2,1)} %bitcast.14, ...), custom_call_target="tpu_custom_call" | custom-call | tf_op jit(solution)/shard_map/pallas_call | solution.py:633
  83.0 1.8 %shard_map.93 = (bf16[192,128]{1,0:T(8,128)(2,1)}, bf16[128,256]{1,0:T(8,128)(2,1)}, bf16[128,256]{1,0:T(8,128)(2,1)}, bf16[128,256]{1,0:T(8,128)(2,1)}, f32[192,128]{1,0:T(8,128)}) custom-call(bf16[192,128]{1,0:T(8,128)(2,1)} %get-tuple-element.15.refs_0_, bf16[128,256]{1,0:T(8,128)(2,1)} %get-tuple-element.16.refs_1_, ...), custom_call_target="tpu_custom_call" | custom-call | tf_op jit(solution)/shard_map/pallas_call | solution.py:686

commit v9 on v6

--- a/solution.py
+++ b/solution.py
@@ -485,10 +485,9 @@
 
     lanes = [slice(h * HEAD, (h + 1) * HEAD) for h in range(2)]
 
-    def project(c, acc):
-        return acc + dot_nt(wf[c], of[lax.rem(c, n) * n + c // n])
-
-    projected = lax.fori_loop(0, n * n, project, jnp.zeros((cols, span), F32))
+    projected = jnp.zeros((cols, span), F32)
+    for c in range(n * n):
+        projected = projected + dot_nt(wf[c], of[c % n * n + c // n])
     for h in range(2):
         ox[h] = projected[:, lanes[h]].astype(BF16)
     o_s = send(ox.at[1 - side], oxr, oxr, twin)

time: 81 us -> 81.1 us (level)
  no operation moved by 1% of the time
where the time goes in v9:
time: 81.1 us; the launch traced here: 80.8 us
  Pallas kernels  80.2 us (99%)
    pallas_call x1, Pallas kernels, shards(): pl.pallas_call(functools.partial(kernel, n, rows, cols), out_shape=(jax.S...  78.4 us
    pallas_call x1, Pallas kernels, shards(): pl.pallas_call(store_all, out_shape=[jax.ShapeDtypeStruct(a.shape, a.dtyp...  1.79 us

profile of v9, /device:TPU:1, one launch (start us, length us, event | category | flops | bytes accessed | tf_op | source)
XLA Modules:
  0.0 80.8 jit_solution(10206683840090249925)
XLA Ops:
  0.6 78.4 %shard_map.92 = (bf16[192,128]{1,0:T(8,128)(2,1)}, bf16[128,256]{1,0:T(8,128)(2,1)}, bf16[128,256]{1,0:T(8,128)(2,1)}, bf16[128,256]{1,0:T(8,128)(2,1)}, f32[192,128]{1,0:T(8,128)}) custom-call(bf16[128,256]{1,0:T(8,128)(2,1)} %bitcast.15, bf16[128,256]{1,0:T(8,128)(2,1)} %bitcast.16, bf16[128,256]{1,0:T(8,128)(2,1)} %bitcast.17, bf16[192,256]{1,0:T(8,128)(2,1)} %bitcast.14, ...), custom_call_target="tpu_custom_call" | custom-call | tf_op jit(solution)/shard_map/pallas_call | solution.py:594
  79.0 1.8 %shard_map.93 = (bf16[192,128]{1,0:T(8,128)(2,1)}, bf16[128,256]{1,0:T(8,128)(2,1)}, bf16[128,256]{1,0:T(8,128)(2,1)}, bf16[128,256]{1,0:T(8,128)(2,1)}, f32[192,128]{1,0:T(8,128)}) custom-call(bf16[192,128]{1,0:T(8,128)(2,1)} %get-tuple-element.15.refs_0_, bf16[128,256]{1,0:T(8,128)(2,1)} %get-tuple-element.16.refs_1_, ...), custom_call_target="tpu_custom_call" | custom-call | tf_op jit(solution)/shard_map/pallas_call | solution.py:645

commit v10 on v9

--- a/solution.py
+++ b/solution.py
@@ -270,6 +270,7 @@
     w_d = {0: send(w_group(y), w_group(y), w_group(y, theirs), dp_peer)}
     q_s = spread_z(qf.at[block(row), :], qs, lambda i: qf.at[block(i), :], z_steps[:1])
     v_z = spread_z(vf.at[block(row), :], vs, lambda i: vf.at[block(i), :], z_steps)
+    q_z = spread_z(qf.at[block(row), :], qs, lambda i: qf.at[block(i), :], z_steps[1:])
     g_s()
     gf[...] = flip(gt[...])
 
@@ -335,7 +336,6 @@
     forward(y, True)
     for d in near:
         head_terms(n - d)
-    q_z = spread_z(qf.at[block(row), :], qs, lambda i: qf.at[block(i), :], z_steps[1:])
     for d in near:
 
         @pl.when(y >= d)

time: 81.1 us -> 80 us (0.986); the launches traced: 80.8 us -> 78.6 us
  Pallas kernels: 80.2 us -> 78 us
    pallas_call x1, Pallas kernels: 78.4 us -> 76.2 us  [shards(): pl.pallas_call(functools.partial(kernel, n, rows, cols), out_shape=(jax.S...]
where the time goes in v10:
time: 80 us; the launch traced here: 78.6 us
  Pallas kernels  78 us (98%)
    pallas_call x1, Pallas kernels, shards(): pl.pallas_call(functools.partial(kernel, n, rows, cols), out_shape=(jax.S...  76.2 us
    pallas_call x1, Pallas kernels, shards(): pl.pallas_call(store_all, out_shape=[jax.ShapeDtypeStruct(a.shape, a.dtyp...  1.79 us

profile of v10, /device:TPU:1, one launch (start us, length us, event | category | flops | bytes accessed | tf_op | source)
XLA Modules:
  0.0 78.6 jit_solution(6293973810397810982)
XLA Ops:
  0.6 76.2 %shard_map.92 = (bf16[192,128]{1,0:T(8,128)(2,1)}, bf16[128,256]{1,0:T(8,128)(2,1)}, bf16[128,256]{1,0:T(8,128)(2,1)}, bf16[128,256]{1,0:T(8,128)(2,1)}, f32[192,128]{1,0:T(8,128)}) custom-call(bf16[128,256]{1,0:T(8,128)(2,1)} %bitcast.15, bf16[128,256]{1,0:T(8,128)(2,1)} %bitcast.16, bf16[128,256]{1,0:T(8,128)(2,1)} %bitcast.17, bf16[192,256]{1,0:T(8,128)(2,1)} %bitcast.14, ...), custom_call_target="tpu_custom_call" | custom-call | tf_op jit(solution)/shard_map/pallas_call | solution.py:594
  76.9 1.8 %shard_map.93 = (bf16[192,128]{1,0:T(8,128)(2,1)}, bf16[128,256]{1,0:T(8,128)(2,1)}, bf16[128,256]{1,0:T(8,128)(2,1)}, bf16[128,256]{1,0:T(8,128)(2,1)}, f32[192,128]{1,0:T(8,128)}) custom-call(bf16[192,128]{1,0:T(8,128)(2,1)} %get-tuple-element.15.refs_0_, bf16[128,256]{1,0:T(8,128)(2,1)} %get-tuple-element.16.refs_1_, ...), custom_call_target="tpu_custom_call" | custom-call | tf_op jit(solution)/shard_map/pallas_call | solution.py:645

commit v11 on v10

--- a/solution.py
+++ b/solution.py
@@ -336,6 +336,7 @@
     forward(y, True)
     for d in near:
         head_terms(n - d)
+    q_y = gather_full(q_z, lambda i: qf.at[span_of(i), :], False)
     for d in near:
 
         @pl.when(y >= d)
@@ -437,7 +438,6 @@
 
     weight_terms(0)
     upstream = head_sums(0)
-    q_y = gather_full(q_z, lambda i: qf.at[span_of(i), :], False)
     if n > 2:
         wait(o_far)
         o_x[2] = spread_x(2)

time: 80 us -> 79.9 us (level)
  no operation moved by 1% of the time
where the time goes in v11:
time: 79.9 us; the launch traced here: 78.6 us
  Pallas kernels  78 us (98%)
    pallas_call x1, Pallas kernels, shards(): pl.pallas_call(functools.partial(kernel, n, rows, cols), out_shape=(jax.S...  76.2 us
    pallas_call x1, Pallas kernels, shards(): pl.pallas_call(store_all, out_shape=[jax.ShapeDtypeStruct(a.shape, a.dtyp...  1.79 us

profile of v11, /device:TPU:1, one launch (start us, length us, event | category | flops | bytes accessed | tf_op | source)
XLA Modules:
  0.0 78.6 jit_solution(14186982052413607334)
XLA Ops:
  0.6 76.2 %shard_map.92 = (bf16[192,128]{1,0:T(8,128)(2,1)}, bf16[128,256]{1,0:T(8,128)(2,1)}, bf16[128,256]{1,0:T(8,128)(2,1)}, bf16[128,256]{1,0:T(8,128)(2,1)}, f32[192,128]{1,0:T(8,128)}) custom-call(bf16[128,256]{1,0:T(8,128)(2,1)} %bitcast.15, bf16[128,256]{1,0:T(8,128)(2,1)} %bitcast.16, bf16[128,256]{1,0:T(8,128)(2,1)} %bitcast.17, bf16[192,256]{1,0:T(8,128)(2,1)} %bitcast.14, ...), custom_call_target="tpu_custom_call" | custom-call | tf_op jit(solution)/shard_map/pallas_call | solution.py:594
  76.8 1.8 %shard_map.93 = (bf16[192,128]{1,0:T(8,128)(2,1)}, bf16[128,256]{1,0:T(8,128)(2,1)}, bf16[128,256]{1,0:T(8,128)(2,1)}, bf16[128,256]{1,0:T(8,128)(2,1)}, f32[192,128]{1,0:T(8,128)}) custom-call(bf16[192,128]{1,0:T(8,128)(2,1)} %get-tuple-element.15.refs_0_, bf16[128,256]{1,0:T(8,128)(2,1)} %get-tuple-element.16.refs_1_, ...), custom_call_target="tpu_custom_call" | custom-call | tf_op jit(solution)/shard_map/pallas_call | solution.py:645
